TPU v7x, 32 devices: a whole 2x2x4 slice. The times are simulated.
32 devices in a mesh: band: 4 (over z), lev: 4 (over y, core), grp: 2 (over x).
Axes of the slice: x: 2, y: 2, z: 4, core: 2. Of those that a mesh axis runs over, the one named last changes fastest.
Arguments:
- fourier: bfloat16 [3, 8, 2, 2, 2, 48, 96], P(None, 'lev', None, None, 'grp', 'band'), may hold values from -6 to 6
- legendre: bfloat16 [96, 2, 48, 2, 48], P('band', None, 'lev', 'grp'), may hold values from -0.625 to 0.625
- lat_points: int32 [2, 48], P('grp', 'band'), may hold values from 20 to 400, as said below
- wave_slots: int32 [96], replicated, may hold values from 0 to 95, as said below
- vertical: float32 [8, 8], replicated, may hold values from -2 to 2
Outputs:
- spectral: bfloat16 [96, 2, 4, 8, 2, 48], P('band', None, None, None, None, ('lev', 'grp'))
Inputs may be any that keep to these rules, and one draw needn't show every extreme that they name: `lat_points`: the values are 20 + 4 i for i = 0 .. 95, each once (octahedral point counts of the latitude pairs, spread over devices). `wave_slots`: every wavenumber appears once; slots 2 i and 2 i + 1 hold wavenumbers m and 95 - m.
All inputs are finite; a program needn't handle non-finite values.
Results may differ from a plain program's by a relative error of at most 0.0053.
Values may be sent and summed in bfloat16 or wider, within the bound.
No kernel may reach another device: no remote copies, remote signals or barrier semaphores. Data moves between devices by JAX's collectives and lax.ppermute only.
A program may use at most 64 MiB of HBM per device.

v0:
```python
import functools

import jax
import jax.numpy as jnp
from jax import lax
from jax.experimental import pallas as pl
from jax.experimental.pallas import tpu as pltpu
from jax.sharding import PartitionSpec as P

F32, BF16 = jnp.float32, jnp.bfloat16
LANES = 128
GRANT = 8 << 20


def flipped(value, axis, step):
    return lax.ppermute(value, axis, [(i, i ^ step) for i in range(lax.axis_size(axis))])


def iota(shape, dim):
    return lax.broadcasted_iota(jnp.int32, shape, dim)


def prepare_kernel(dims, lat_hbm, slots_hbm, x_hbm, functions_hbm, vertical_hbm, slot_lanes_ref, functions_ref, vertical_ref, *rest):
    fields, planes, pairs, slots, waves = dims
    block_refs, (lat_ref, slots_ref, x_ref, sems) = rest[:-4], rest[-4:]
    width = LANES // planes
    band = lax.axis_index("band")
    copies = [
        pltpu.make_async_copy(source, target, sems.at[i])
        for i, (source, target) in enumerate(
            (
                (slots_hbm, slots_ref),
                (lat_hbm, lat_ref),
                (x_hbm, x_ref),
                (functions_hbm, functions_ref),
                (vertical_hbm, vertical_ref),
            )
        )
    ]
    for copy in copies:
        copy.start()
    lane = iota((8, LANES), 1)
    copies[0].wait()
    tables = []
    for k in range(len(block_refs)):
        first = (band ^ k) * slots
        held = jnp.full((8, LANES), -1, jnp.int32)
        for s in range(slots):
            held = jnp.where(lane % width == s, slots_ref[0, first + s], held)
        if k == 0:
            slot_lanes_ref[...] = held
        hot = iota((waves, LANES), 0) == held[0:1]
        tables.append(jnp.where(hot, 1.0, 0.0).astype(BF16))
    pair_rows = iota((2 * pairs, waves), 0) // 2
    cutoff = jnp.zeros((2 * pairs, waves), jnp.int32)
    copies[1].wait()
    for q in range(pairs):
        cutoff = jnp.where(pair_rows == q, jnp.minimum(waves - 1, (lat_ref[0, q] - 1) // 2), cutoff)
    kept = iota((2 * pairs, waves), 1) <= cutoff
    copies[2].wait()
    x = x_ref[...].astype(F32)
    rows = x.shape[0]
    following = pltpu.roll(x, rows - 1, 0)
    previous = pltpu.roll(x, 1, 0)
    north = (iota(x.shape, 0) & 1) == 0
    parity = jnp.where(north, x + following, previous - x)
    parity = parity.reshape(fields * planes, 2 * pairs, waves)
    parity = jnp.where(kept[None], parity, 0.0)
    by_plane = jnp.concatenate(
        [parity[f * planes + plane] for plane in range(planes) for f in range(fields)], axis=0
    ).astype(BF16)
    chosen = jnp.dot(by_plane, jnp.concatenate(tables, axis=1), preferred_element_type=F32)
    count = 2 * fields * pairs
    plane_of = iota((count, LANES), 1) // width
    for k, block_ref in enumerate(block_refs):
        mine = chosen[:, k * LANES : (k + 1) * LANES]
        block = mine[:count]
        for plane in range(1, planes):
            block = jnp.where(plane_of == plane, mine[plane * count : (plane + 1) * count], block)
        block_ref[...] = block.astype(BF16)
    copies[3].wait()
    copies[4].wait()


def spread_kernel(dims, own_ref, other_ref, vertical_ref, out_ref, weights_ref, rows_ref):
    planes, slots, halves, sums = dims
    width = LANES // planes
    group = lax.axis_index("grp")
    block = iota((sums, LANES), 1) // width
    own = halves // 2
    levels = vertical_ref.shape[0]
    for level in range(levels):
        for k in range(level, levels):
            weights_ref[level * levels + k] = jnp.broadcast_to(vertical_ref[level : level + 1, k : k + 1], (8, LANES))
    for side, ref in enumerate((own_ref, other_ref)):
        rows_ref[side, :, :sums] = ref[...].astype(F32)
        for p in range(2):
            for first in range(0, halves, planes):
                pieces = []
                for part in range(planes):
                    start = (first + part) * 2 + p
                    pieces.append(rows_ref[side, pl.ds(start, slots, stride=2 * halves), :])
                    if width > slots:
                        pieces.append(jnp.zeros((width - slots, LANES), F32))
                turned = jnp.concatenate(pieces, axis=0).T[:sums]
                rolled = [turned] + [pltpu.roll(turned, d * width, 1) for d in range(1, planes)]
                for part in range(planes):
                    copies = rolled[-part % planes]
                    for plane in range(1, planes):
                        copies = jnp.where(block == plane, rolled[(plane - part) % planes], copies)
                    j = first + part
                    jj = j % own
                    if side == 0:
                        here, there = (jj // 2) * 8 + 6 + jj % 2, jj
                    else:
                        here, there = 8 + jj, 16 + jj
                    start = jnp.where(group == j // own, here, there)
                    out_ref[p, pl.ds(start, sums, stride=24), :] = copies


def sum_kernel(dims, *refs):
    fields, pairs, bands = dims
    blocks, (table_ref, total_ref, x_ref, y_ref, xy_ref, rows_ref) = refs[: 2 * bands], refs[2 * bands :]
    band = lax.axis_index("band")
    for i, block in enumerate(blocks):
        rows_ref[i] = block[...].astype(F32)
    for p in range(2):
        totals = [jnp.zeros((24, LANES), F32) for _ in range(2 * fields)]
        for k in range(bands):
            first = (band ^ k) * pairs
            for q in range(pairs):
                factors = table_ref[p, pl.ds(pl.multiple_of((first + q) * 24, 8), 24), :]
                for side in range(2):
                    for f in range(fields):
                        row = (f * pairs + q) * 2 + p
                        i = side * fields + f
                        totals[i] += rows_ref[side * bands + k, row : row + 1, :] * factors
        for i, total in enumerate(totals):
            total_ref[2 * i + p] = total
    for at, ref in ((0, x_ref), (8, y_ref), (16, xy_ref)):
        ref[...] = total_ref[:, at : at + 8, :].reshape(ref.shape).astype(BF16)


def finish_kernel(dims, weights_ref, slot_lanes_ref, total_ref, x_ref, y_ref, xy_ref, out_ref, temps_ref, rows_ref):
    fields, levels, halves, slots, waves = dims
    planes = 2 * (levels // 4)
    width = LANES // planes
    lev, group = lax.axis_index("lev"), lax.axis_index("grp")
    y, core = lev // 2, lev % 2
    count = 4 * fields
    from_x, from_y, from_xy = (r[...].astype(F32).reshape(count, 8, LANES) for r in (x_ref, y_ref, xy_ref))
    half = (lev * 2 + group) * halves + iota((8, LANES), 0)
    valid = [slot_lanes_ref[...] + 2 * half + p <= waves - 1 for p in range(2)]

    def store(p, f, level, c, value):
        start = ((p * (fields + 1) + f) * levels + level) * (2 * halves) + c
        rows_ref[pl.ds(start, halves, stride=2), :] = value[:halves]

    for side in range(2):
        for f in range(fields):
            for p in range(2):
                n = (side * fields + f) * 2 + p
                kept = jnp.concatenate(
                    [total_ref[n, 6:8, :], total_ref[n, 14:16, :], total_ref[n, 22:24, :], jnp.zeros((2, LANES), F32)],
                    axis=0,
                )
                for far, value in enumerate((kept + from_x[n], from_y[n] + from_xy[n])):
                    value = jnp.where(valid[p], value, 0.0)
                    first = ((y ^ far) * 2 + (core ^ side)) * (levels // 4)
                    for plane in range(planes):
                        l, c = plane // 2, plane % 2
                        shifted = value if plane == 0 else pltpu.roll(value, LANES - plane * width, 1)
                        store(p, f, first + l, c, shifted)
                        if f == fields - 1:
                            temps_ref[first + l, 2 * p + c] = shifted
    for p in range(2):
        for c in range(2):
            temps = [temps_ref[k, 2 * p + c] for k in range(levels)]
            for level in range(levels):
                value = weights_ref[level * levels + level] * temps[level]
                for k in range(level + 1, levels):
                    value += weights_ref[level * levels + k] * temps[k]
                store(p, fields, level, c, value)
    out_ref[...] = rows_ref[:, :slots].astype(BF16)


HBM = pl.BlockSpec(memory_space=pltpu.HBM)
VMEM = pl.BlockSpec(memory_space=pltpu.VMEM)


def fast_body(fourier, legendre, lat_points, wave_slots, vertical):
    fields, local_levels, _, _, _, pairs, waves = fourier.shape
    slots, _, halves, _, sums = legendre.shape
    bands = lax.axis_size("band")
    levels = 4 * local_levels
    planes = 2 * local_levels
    shape = jax.ShapeDtypeStruct

    functions = legendre.transpose(0, 2, 3, 1, 4).reshape(slots * halves * 2, sums)
    other_functions = flipped(functions, "lev", 2)

    rows = fourier.transpose(0, 1, 2, 4, 5, 3, 6).reshape(-1, waves)
    block = shape((2 * fields * pairs, LANES), BF16)
    slot_lanes, functions, vertical, *blocks = pl.pallas_call(
        functools.partial(prepare_kernel, (fields, planes, pairs, slots, waves)),
        in_specs=[HBM] * 5,
        out_specs=[VMEM] * (3 + bands),
        out_shape=[
            shape((8, LANES), jnp.int32),
            shape(functions.shape, BF16),
            shape(vertical.shape, F32),
        ]
        + [block] * bands,
        scratch_shapes=[
            pltpu.SMEM(lat_points.shape, jnp.int32),
            pltpu.SMEM((1, wave_slots.size), jnp.int32),
            pltpu.VMEM(rows.shape, BF16),
            pltpu.SemaphoreType.DMA((5,)),
        ],
        compiler_params=pltpu.CompilerParams(vmem_limit_bytes=GRANT),
        name="prepare",
    )(*[pltpu.with_memory_space_constraint(v, pltpu.HBM) for v in (lat_points, wave_slots.reshape(1, -1), rows, functions, vertical)])

    far = tuple(reversed(range(1, bands)))
    own = {0: blocks[0]}
    for k in far:
        own[k] = flipped(blocks[k], "band", k)
    table, weights = pl.pallas_call(
        functools.partial(spread_kernel, (planes, slots, halves, sums)),
        in_specs=[VMEM] * 3,
        out_specs=[VMEM] * 2,
        out_shape=[shape((2, sums * 24, LANES), F32), shape((levels * levels, 8, LANES), F32)],
        scratch_shapes=[pltpu.VMEM((2, slots * halves * 2, LANES), F32)],
        compiler_params=pltpu.CompilerParams(vmem_limit_bytes=GRANT),
        name="spread",
    )(functions, other_functions, vertical)
    other = {}
    for k in (0, *far):
        other[k] = flipped(own[k], "lev", 1)

    count = 4 * fields
    message = shape((count * 8, LANES), BF16)
    total, to_x, to_y, to_xy = pl.pallas_call(
        functools.partial(sum_kernel, (fields, pairs, bands)),
        in_specs=[VMEM] * (2 * bands + 1),
        out_specs=[VMEM] * 4,
        out_shape=[shape((count, 24, LANES), F32)] + [message] * 3,
        scratch_shapes=[pltpu.VMEM((2 * bands, *block.shape), F32)],
        compiler_params=pltpu.CompilerParams(vmem_limit_bytes=GRANT),
        name="sum",
    )(*[own[k] for k in range(bands)], *[other[k] for k in range(bands)], table)

    from_xy = lax.ppermute(to_xy, ("lev", "grp"), [(i, i ^ 5) for i in range(8)])
    from_x = flipped(to_x, "grp", 1)
    from_y = flipped(to_y, "lev", 2)
    own_halves = halves // 2
    out_rows = 2 * (fields + 1) * levels * own_halves * 2
    out = pl.pallas_call(
        functools.partial(finish_kernel, (fields, levels, own_halves, slots, waves)),
        in_specs=[VMEM] * 6,
        out_specs=VMEM,
        out_shape=shape((out_rows, slots), BF16),
        scratch_shapes=[pltpu.VMEM((levels, 4, 8, LANES), F32), pltpu.VMEM((out_rows, LANES), F32)],
        compiler_params=pltpu.CompilerParams(vmem_limit_bytes=GRANT),
        name="finish",
    )(weights, slot_lanes, total, from_x, from_y, from_xy)
    out = out.reshape(2, fields + 1, levels, own_halves, 2, slots)
    return out.transpose(5, 0, 1, 2, 4, 3)


def fits(mesh, fourier, legendre):
    bands, levs, groups = (mesh.shape[a] for a in ("band", "lev", "grp"))
    _, levels, _, _, _, pairs, waves = fourier.shape
    slots, _, halves, _, sums = legendre.shape
    planes = 2 * levels // levs
    return (
        levs == 4
        and groups == 2
        and bands & (bands - 1) == 0
        and waves <= LANES
        and sums <= LANES
        and halves // levs == 12
        and LANES % planes == 0
        and 12 % planes == 0
        and slots // bands <= LANES // planes
        and slots // bands % 8 == 0
        and 2 * pairs // bands % 8 == 0
        and sums % 8 == 0
    )


def general_body(fourier, legendre, lat_points, wave_slots, vertical):
    wave_count = fourier.shape[6]
    cutoff = jnp.minimum(wave_count - 1, (lat_points - 1) // 2)
    wave_ids = lax.broadcasted_iota(jnp.int32, (1, 1, wave_count), 2)
    kept_mask = wave_ids <= cutoff[:, :, None]
    masked = jnp.where(kept_mask, fourier, jnp.zeros((), fourier.dtype))
    slot_table = (
        wave_slots[:, None] == lax.broadcasted_iota(jnp.int32, (wave_count, wave_count), 1)
    ).astype(jnp.bfloat16)
    ordered = lax.dot_general(
        slot_table, masked, (((1,), (6,)), ((), ())), preferred_element_type=jnp.float32
    ).astype(jnp.bfloat16)
    at_owners = lax.all_to_all(ordered, "band", split_axis=0, concat_axis=6, tiled=True)
    coeffs = lax.all_gather(at_owners, "lev", axis=2, tiled=True)
    level_count = coeffs.shape[2]
    level_rows = lax.broadcasted_iota(jnp.int32, (level_count, level_count), 0)
    level_cols = lax.broadcasted_iota(jnp.int32, (level_count, level_count), 1)
    integral = jnp.where(level_cols >= level_rows, vertical, jnp.zeros((), vertical.dtype))
    geopotential = jnp.einsum(
        "lk,skchgr->slchgr",
        integral,
        coeffs[:, 2].astype(jnp.float32),
        precision=lax.Precision.HIGHEST,
    ).astype(jnp.bfloat16)
    fields = jnp.concatenate([coeffs, geopotential[:, None]], axis=1)
    northern = fields[:, :, :, :, 0].astype(jnp.float32)
    southern = fields[:, :, :, :, 1].astype(jnp.float32)
    parity = jnp.stack(
        [(northern + southern).astype(jnp.bfloat16), (northern - southern).astype(jnp.bfloat16)],
        axis=4,
    )
    partial_value = lax.dot_general(
        parity, legendre, (((5, 6), (3, 4)), ((0, 4), (0, 1))), preferred_element_type=jnp.float32
    )
    groups = lax.axis_size("grp")
    half_count = partial_value.shape[5] // groups
    me = lax.axis_index("grp")
    summed = lax.dynamic_slice_in_dim(partial_value, me * half_count, half_count, 5)
    for step in range(1, groups):
        target = lax.rem(me + step, groups)
        piece = lax.dynamic_slice_in_dim(partial_value, target * half_count, half_count, 5)
        summed = summed + lax.ppermute(
            piece, "grp", [(i, (i + step) % groups) for i in range(groups)]
        )
    slot_count = summed.shape[0]
    slot_waves = lax.dynamic_slice_in_dim(
        wave_slots, lax.axis_index("band") * slot_count, slot_count
    )
    block_start = (lax.axis_index("lev") * groups + me) * half_count
    half_ids = block_start + lax.broadcasted_iota(jnp.int32, (1, 1, half_count), 2)
    parity_ids = lax.broadcasted_iota(jnp.int32, (1, 2, 1), 1)
    total = slot_waves[:, None, None] + 2 * half_ids + parity_ids
    valid = (total <= wave_count - 1)[:, :, None, None, None, :]
    return jnp.where(valid, summed, 0.0).astype(jnp.bfloat16)


def solution(mesh):
    def program(fourier, legendre, lat_points, wave_slots, vertical):
        placed = (
            P(None, "lev", None, None, "grp", "band", None),
            P("band", None, "lev", "grp", None),
            P("grp", "band"),
            P(),
            P(),
        )
        fast = fits(mesh, fourier, legendre)
        step = jax.shard_map(
            fast_body if fast else general_body,
            mesh=mesh,
            in_specs=placed,
            out_specs=P("band", None, None, None, None, ("lev", "grp")),
            check_vma=False,
        )
        return step(fourier, legendre, lat_points, wave_slots, vertical)

    return program
```

profile of v0, /device:TPU:0, one launch (start us, length us, event | category | flops | bytes accessed | tf_op | source)
XLA Modules:
  0.0 22.4 jit_solution(14040711101069592463)
XLA Ops:
  0.0 3.0 %collective-permute-start = (bf16[576,48]{1,0:T(8,128)(2,1)}, bf16[576,48]{1,0:T(8,128)(2,1)S(1)}, u32[]{:S(2)}, u32[]{:S(2)}) collective-permute-start(bf16[576,48]{1,0:T(8,128)(2,1)} %bitcast.10), channel_id=1, source_target_pairs={{0,4},{2,6},{4,0},{6,2},{1,5},{3,7},{5,1},{7,3},{8,12},{10,14},{12... | collective-permute-start | bytes 165896 | tf_op jit(solution)/shard_map/ppermute | solution.py:16
  3.0 1.2 %prepare.1 = (s32[8,128]{1,0:T(8,128)S(1)}, bf16[576,48]{1,0:T(8,128)(2,1)S(1)}, f32[8,8]{1,0:T(8,128)S(1)}, bf16[72,128]{1,0:T(8,128)(2,1)S(1)}, bf16[72,128]{1...) custom-call(s32[1,12]{1,0:T(1,128)} %lat_hbm.1, s32[1,96]{1,0:T(1,128)} %bitcast.13, ...), custom_call_target="tpu_custom_call" | custom-call | tf_op jit(solution)/shard_map/prepare/pallas_call | solution.py:204
  4.2 1.6 %collective-permute-start.1 = (bf16[72,128]{1,0:T(8,128)(2,1)S(1)}, bf16[72,128]{1,0:T(8,128)(2,1)S(1)}, u32[]{:S(2)}, u32[]{:S(2)}) collective-permute-start(bf16[72,128]{1,0:T(8,128)(2,1)S(1)} %get-tuple-element.23), channel_id=1, source_target_pairs={{0,8},{8,0},{16,24},{24,16},{1,9},{9,1},{17,25},{25,17},{2,10},{10... | collective-permute-start | bytes 55304 | tf_op jit(solution)/shard_map/ppermute | solution.py:16
  5.8 2.6 %collective-permute-start.2 = (bf16[72,128]{1,0:T(8,128)(2,1)S(1)}, bf16[72,128]{1,0:T(8,128)(2,1)S(1)}, u32[]{:S(2)}, u32[]{:S(2)}) collective-permute-start(bf16[72,128]{1,0:T(8,128)(2,1)S(1)} %get-tuple-element.24), channel_id=1, source_target_pairs={{0,16},{8,24},{16,0},{24,8},{1,17},{9,25},{17,1},{25,9},{2,18},{10... | collective-permute-start | bytes 55304 | tf_op jit(solution)/shard_map/ppermute | solution.py:16
  8.4 0.2 collective-permute-start.3
  8.6 0.0 collective-permute-start.4
  8.6 0.0 collective-permute-done.1.refs_1_
  8.6 0.5 %collective-permute-start.5 = (bf16[72,128]{1,0:T(8,128)(2,1)S(1)}, bf16[72,128]{1,0:T(8,128)(2,1)S(1)}, u32[]{:S(2)}, u32[]{:S(2)}) collective-permute-start(bf16[72,128]{1,0:T(8,128)(2,1)S(1)} %collective-permute-done.1.refs_1_), channel_id=1, source_target_pairs={{0,2},{2,0},{4,6},{6,4},{1,3},{3,1},{5,7},{7,5},{8,10},{10,8},{12,... | collective-permute-start | bytes 55304 | tf_op jit(solution)/shard_map/ppermute | solution.py:16
  9.1 1.4 %collective-permute-done.2.refs_2_ = bf16[72,128]{1,0:T(8,128)(2,1)S(1)} collective-permute-done((bf16[72,128]{1,0:T(8,128)(2,1)S(1)}, bf16[72,128]{1,0:T(8,128)(2,1)S(1)}, u32[]{:S(2)}, u32[]{:S(2)}) %collective-permute-start.2) | collective-permute-done | bytes 18464 | tf_op jit(solution)/shard_map/ppermute | solution.py:16
  10.5 0.0 collective-permute-start.6
  10.5 3.4 %collective-permute-done.3.refs_3_ = bf16[72,128]{1,0:T(8,128)(2,1)S(1)} collective-permute-done((bf16[72,128]{1,0:T(8,128)(2,1)S(1)}, bf16[72,128]{1,0:T(8,128)(2,1)S(1)}, u32[]{:S(2)}, u32[]{:S(2)}) %collective-permute-start.3) | collective-permute-done | bytes 18464 | tf_op jit(solution)/shard_map/ppermute | solution.py:16
  14.0 0.0 collective-permute-start.7
  14.0 0.0 collective-permute-done.other_ref
  14.0 0.6 %spread.1 = (f32[2,1152,128]{2,1,0:T(8,128)S(1)}, f32[64,8,128]{2,1,0:T(8,128)S(1)}) custom-call(bf16[576,48]{1,0:T(8,128)(2,1)S(1)} %get-tuple-element.18.own_ref, bf16[576,48]{1,0:T(8,128)(2,1)S(1)} %collective-permute-done.other_ref, f32[8,8]{1,0:T(8,128)S(1)} %get-tuple-element.19.vertical_ref), custom_call_target="tpu_custom_call" | custom-call | tf_op jit(solution)/shard_map/spread/pallas_call | solution.py:228
  14.6 0.0 collective-permute-done.4.refs_4_
  14.6 0.0 collective-permute-done.5.refs_5_
  14.6 0.0 collective-permute-done.6.refs_6_
  14.6 0.5 %collective-permute-done.7.refs_7_ = bf16[72,128]{1,0:T(8,128)(2,1)S(1)} collective-permute-done((bf16[72,128]{1,0:T(8,128)(2,1)S(1)}, bf16[72,128]{1,0:T(8,128)(2,1)S(1)}, u32[]{:S(2)}, u32[]{:S(2)}) %collective-permute-start.7) | collective-permute-done | bytes 18464 | tf_op jit(solution)/shard_map/ppermute | solution.py:16
  15.1 0.5 %sum.1 = (f32[12,24,128]{2,1,0:T(8,128)S(1)}, bf16[96,128]{1,0:T(8,128)(2,1)S(1)}, bf16[96,128]{1,0:T(8,128)(2,1)S(1)}, bf16[96,128]{1,0:T(8,128)(2,1)S(1)}) custom-call(bf16[72,128]{1,0:T(8,128)(2,1)S(1)} %get-tuple-element.22.refs_0_, bf16[72,128]{1,0:T(8,128)(2,1)S(1)} %collective-permute-done.1.refs_1_, ...), custom_call_target="tpu_custom_call" | custom-call | tf_op jit(solution)/shard_map/sum/pallas_call | solution.py:243
  15.7 1.5 %collective-permute-start.10 = (bf16[96,128]{1,0:T(8,128)(2,1)S(1)}, bf16[96,128]{1,0:T(8,128)(2,1)S(1)}, u32[]{:S(2)}, u32[]{:S(2)}) collective-permute-start(bf16[96,128]{1,0:T(8,128)(2,1)S(1)} %get-tuple-element.30), channel_id=1, source_target_pairs={{0,5},{1,4},{2,7},{3,6},{4,1},{5,0},{6,3},{7,2},{8,13},{9,12},{10,... | collective-permute-start | bytes 73736 | tf_op jit(solution)/shard_map/ppermute | solution.py:253
  17.2 0.5 %collective-permute-start.8 = (bf16[96,128]{1,0:T(8,128)(2,1)S(1)}, bf16[96,128]{1,0:T(8,128)(2,1)S(1)}, u32[]{:S(2)}, u32[]{:S(2)}) collective-permute-start(bf16[96,128]{1,0:T(8,128)(2,1)S(1)} %get-tuple-element.28), channel_id=1, source_target_pairs={{0,1},{1,0},{2,3},{3,2},{4,5},{5,4},{6,7},{7,6},{8,9},{9,8},{10,11... | collective-permute-start | bytes 73736 | tf_op jit(solution)/shard_map/ppermute | solution.py:16
  17.7 1.5 %collective-permute-start.9 = (bf16[96,128]{1,0:T(8,128)(2,1)S(1)}, bf16[96,128]{1,0:T(8,128)(2,1)S(1)}, u32[]{:S(2)}, u32[]{:S(2)}) collective-permute-start(bf16[96,128]{1,0:T(8,128)(2,1)S(1)} %get-tuple-element.29), channel_id=1, source_target_pairs={{0,4},{2,6},{4,0},{6,2},{1,5},{3,7},{5,1},{7,3},{8,12},{10,14},{12... | collective-permute-start | bytes 73736 | tf_op jit(solution)/shard_map/ppermute | solution.py:16
  19.2 1.2 %collective-permute-done.10.xy_ref = bf16[96,128]{1,0:T(8,128)(2,1)S(1)} collective-permute-done((bf16[96,128]{1,0:T(8,128)(2,1)S(1)}, bf16[96,128]{1,0:T(8,128)(2,1)S(1)}, u32[]{:S(2)}, u32[]{:S(2)}) %collective-permute-start.10) | collective-permute-done | bytes 24608 | tf_op jit(solution)/shard_map/ppermute | solution.py:253
  20.4 0.5 %collective-permute-done.8.x_ref = bf16[96,128]{1,0:T(8,128)(2,1)S(1)} collective-permute-done((bf16[96,128]{1,0:T(8,128)(2,1)S(1)}, bf16[96,128]{1,0:T(8,128)(2,1)S(1)}, u32[]{:S(2)}, u32[]{:S(2)}) %collective-permute-start.8) | collective-permute-done | bytes 24608 | tf_op jit(solution)/shard_map/ppermute | solution.py:16
  21.0 0.5 %collective-permute-done.9.y_ref = bf16[96,128]{1,0:T(8,128)(2,1)S(1)} collective-permute-done((bf16[96,128]{1,0:T(8,128)(2,1)S(1)}, bf16[96,128]{1,0:T(8,128)(2,1)S(1)}, u32[]{:S(2)}, u32[]{:S(2)}) %collective-permute-start.9) | collective-permute-done | bytes 24608 | tf_op jit(solution)/shard_map/ppermute | solution.py:16
  21.5 0.9 %finish.1 = bf16[768,24]{1,0:T(8,128)(2,1)} custom-call(f32[64,8,128]{2,1,0:T(8,128)S(1)} %get-tuple-element.20.weights_ref, s32[8,128]{1,0:T(8,128)S(1)} %get-tuple-element.21.slot_lanes_ref, f32[12,24,128]{2,1,0:T(8,128)S(1)} %get-tuple-element.27.total_ref, bf16[96,128]{1,0:T(8,128)(2,1)S(1)} %collective-permute-done.8.x_ref, ...), custom_call_target="tpu_custom_call" | custom-call | tf_op jit(solution)/shard_map/finish/pallas_call | solution.py:258
Async XLA Ops:
  0.0 14.0 %collective-permute-start = (bf16[576,48]{1,0:T(8,128)(2,1)}, bf16[576,48]{1,0:T(8,128)(2,1)S(1)}, u32[]{:S(2)}, u32[]{:S(2)}) collective-permute-start(bf16[576,48]{1,0:T(8,128)(2,1)} %bitcast.10), channel_id=1, source_target_pairs={{0,4},{2,6},{4,0},{6,2},{1,5},{3,7},{5,1},{7,3},{8,12},{10,14},{12... | collective-permute-start | bytes 165896 | tf_op jit(solution)/shard_map/ppermute | solution.py:16
  4.2 4.5 %collective-permute-start.1 = (bf16[72,128]{1,0:T(8,128)(2,1)S(1)}, bf16[72,128]{1,0:T(8,128)(2,1)S(1)}, u32[]{:S(2)}, u32[]{:S(2)}) collective-permute-start(bf16[72,128]{1,0:T(8,128)(2,1)S(1)} %get-tuple-element.23), channel_id=1, source_target_pairs={{0,8},{8,0},{16,24},{24,16},{1,9},{9,1},{17,25},{25,17},{2,10},{10... | collective-permute-start | bytes 55304 | tf_op jit(solution)/shard_map/ppermute | solution.py:16
  5.8 4.7 %collective-permute-start.2 = (bf16[72,128]{1,0:T(8,128)(2,1)S(1)}, bf16[72,128]{1,0:T(8,128)(2,1)S(1)}, u32[]{:S(2)}, u32[]{:S(2)}) collective-permute-start(bf16[72,128]{1,0:T(8,128)(2,1)S(1)} %get-tuple-element.24), channel_id=1, source_target_pairs={{0,16},{8,24},{16,0},{24,8},{1,17},{9,25},{17,1},{25,9},{2,18},{10... | collective-permute-start | bytes 55304 | tf_op jit(solution)/shard_map/ppermute | solution.py:16
  8.4 5.6 %collective-permute-start.3 = (bf16[72,128]{1,0:T(8,128)(2,1)S(1)}, bf16[72,128]{1,0:T(8,128)(2,1)S(1)}, u32[]{:S(2)}, u32[]{:S(2)}) collective-permute-start(bf16[72,128]{1,0:T(8,128)(2,1)S(1)} %get-tuple-element.25), channel_id=1, source_target_pairs={{0,24},{8,16},{16,8},{24,0},{1,25},{9,17},{17,9},{25,1},{2,26},{10... | collective-permute-start | bytes 55304 | tf_op jit(solution)/shard_map/ppermute | solution.py:16
  8.6 6.0 %collective-permute-start.4 = (bf16[72,128]{1,0:T(8,128)(2,1)S(1)}, bf16[72,128]{1,0:T(8,128)(2,1)S(1)}, u32[]{:S(2)}, u32[]{:S(2)}) collective-permute-start(bf16[72,128]{1,0:T(8,128)(2,1)S(1)} %get-tuple-element.22.refs_0_), channel_id=1, source_target_pairs={{0,2},{2,0},{4,6},{6,4},{1,3},{3,1},{5,7},{7,5},{8,10},{10,8},{12,... | collective-permute-start | bytes 55304 | tf_op jit(solution)/shard_map/ppermute | solution.py:16
  8.6 6.0 %collective-permute-start.5 = (bf16[72,128]{1,0:T(8,128)(2,1)S(1)}, bf16[72,128]{1,0:T(8,128)(2,1)S(1)}, u32[]{:S(2)}, u32[]{:S(2)}) collective-permute-start(bf16[72,128]{1,0:T(8,128)(2,1)S(1)} %collective-permute-done.1.refs_1_), channel_id=1, source_target_pairs={{0,2},{2,0},{4,6},{6,4},{1,3},{3,1},{5,7},{7,5},{8,10},{10,8},{12,... | collective-permute-start | bytes 55304 | tf_op jit(solution)/shard_map/ppermute | solution.py:16
  10.5 4.1 %collective-permute-start.6 = (bf16[72,128]{1,0:T(8,128)(2,1)S(1)}, bf16[72,128]{1,0:T(8,128)(2,1)S(1)}, u32[]{:S(2)}, u32[]{:S(2)}) collective-permute-start(bf16[72,128]{1,0:T(8,128)(2,1)S(1)} %collective-permute-done.2.refs_2_), channel_id=1, source_target_pairs={{0,2},{2,0},{4,6},{6,4},{1,3},{3,1},{5,7},{7,5},{8,10},{10,8},{12,... | collective-permute-start | bytes 55304 | tf_op jit(solution)/shard_map/ppermute | solution.py:16
  14.0 1.2 %collective-permute-start.7 = (bf16[72,128]{1,0:T(8,128)(2,1)S(1)}, bf16[72,128]{1,0:T(8,128)(2,1)S(1)}, u32[]{:S(2)}, u32[]{:S(2)}) collective-permute-start(bf16[72,128]{1,0:T(8,128)(2,1)S(1)} %collective-permute-done.3.refs_3_), channel_id=1, source_target_pairs={{0,2},{2,0},{4,6},{6,4},{1,3},{3,1},{5,7},{7,5},{8,10},{10,8},{12,... | collective-permute-start | bytes 55304 | tf_op jit(solution)/shard_map/ppermute | solution.py:16
  15.7 4.8 %collective-permute-start.10 = (bf16[96,128]{1,0:T(8,128)(2,1)S(1)}, bf16[96,128]{1,0:T(8,128)(2,1)S(1)}, u32[]{:S(2)}, u32[]{:S(2)}) collective-permute-start(bf16[96,128]{1,0:T(8,128)(2,1)S(1)} %get-tuple-element.30), channel_id=1, source_target_pairs={{0,5},{1,4},{2,7},{3,6},{4,1},{5,0},{6,3},{7,2},{8,13},{9,12},{10,... | collective-permute-start | bytes 73736 | tf_op jit(solution)/shard_map/ppermute | solution.py:253
  17.2 3.8 %collective-permute-start.8 = (bf16[96,128]{1,0:T(8,128)(2,1)S(1)}, bf16[96,128]{1,0:T(8,128)(2,1)S(1)}, u32[]{:S(2)}, u32[]{:S(2)}) collective-permute-start(bf16[96,128]{1,0:T(8,128)(2,1)S(1)} %get-tuple-element.28), channel_id=1, source_target_pairs={{0,1},{1,0},{2,3},{3,2},{4,5},{5,4},{6,7},{7,6},{8,9},{9,8},{10,11... | collective-permute-start | bytes 73736 | tf_op jit(solution)/shard_map/ppermute | solution.py:16
  17.7 3.8 %collective-permute-start.9 = (bf16[96,128]{1,0:T(8,128)(2,1)S(1)}, bf16[96,128]{1,0:T(8,128)(2,1)S(1)}, u32[]{:S(2)}, u32[]{:S(2)}) collective-permute-start(bf16[96,128]{1,0:T(8,128)(2,1)S(1)} %get-tuple-element.29), channel_id=1, source_target_pairs={{0,4},{2,6},{4,0},{6,2},{1,5},{3,7},{5,1},{7,3},{8,12},{10,14},{12... | collective-permute-start | bytes 73736 | tf_op jit(solution)/shard_map/ppermute | solution.py:16
where the time goes:
time: 22.6 us; the launch traced here: 22.4 us
  starting transfers between devices  11.5 us (51%)
  waiting for transfers between devices  7.67 us (34%)
  Pallas kernels  3.17 us (14%)
    ppermute x10, starting transfers between devices, flipped(): lax.ppermute(value, axis, [(i, i ^ step) for i in range(lax.axis_size(axi...  10 us
    ppermute x10, waiting for transfers between devices, flipped(): lax.ppermute(value, axis, [(i, i ^ step) for i in range(lax.axis_size(axi...  6.43 us
    ppermute x1, starting transfers between devices, fast_body(): lax.ppermute(to_xy, ('lev', 'grp'), [(i, i ^ 5) for i in range(8)])  1.5 us
    ppermute x1, waiting for transfers between devices, fast_body(): lax.ppermute(to_xy, ('lev', 'grp'), [(i, i ^ 5) for i in range(8)])  1.24 us
    pallas_call x1, Pallas kernels, fast_body(): pl.pallas_call(functools.partial(prepare_kernel, (fields, planes, pairs,...  1.16 us
    pallas_call x1, Pallas kernels, fast_body(): pl.pallas_call(functools.partial(finish_kernel, (fields, levels, own_halv...  0.89 us
    pallas_call x1, Pallas kernels, fast_body(): pl.pallas_call(functools.partial(spread_kernel, (planes, slots, halves, s...  0.62 us
    pallas_call x1, Pallas kernels, fast_body(): pl.pallas_call(functools.partial(sum_kernel, (fields, pairs, bands)), in_...  0.51 us
  transfers between devices with their start and end apart: 11, of which 6 were waited for; matrix products, arithmetic and copies ran while one was open for 0% of the time, Pallas kernels for 8%

commit v1 on v0

--- a/solution.py
+++ b/solution.py
@@ -14,6 +14,11 @@
 
 def flipped(value, axis, step):
     return lax.ppermute(value, axis, [(i, i ^ step) for i in range(lax.axis_size(axis))])
+
+
+def crossed(step):
+    bands, levs = lax.axis_size("band"), lax.axis_size("lev")
+    return [(b * levs + v, (b + step) % bands * levs + (v ^ 1)) for b in range(bands) for v in range(levs)]
 
 
 def iota(shape, dim):
@@ -43,7 +48,7 @@
     copies[0].wait()
     tables = []
     for k in range(len(block_refs)):
-        first = (band ^ k) * slots
+        first = lax.rem(band + k, len(block_refs)) * slots
         held = jnp.full((8, LANES), -1, jnp.int32)
         for s in range(slots):
             held = jnp.where(lane % width == s, slots_ref[0, first + s], held)
@@ -127,7 +132,7 @@
     for p in range(2):
         totals = [jnp.zeros((24, LANES), F32) for _ in range(2 * fields)]
         for k in range(bands):
-            first = (band ^ k) * pairs
+            first = lax.rem(band + bands - k, bands) * pairs
             for q in range(pairs):
                 factors = table_ref[p, pl.ds(pl.multiple_of((first + q) * 24, 8), 24), :]
                 for side in range(2):
@@ -160,11 +165,12 @@
         for f in range(fields):
             for p in range(2):
                 n = (side * fields + f) * 2 + p
+                far_n = ((1 - side) * fields + f) * 2 + p
                 kept = jnp.concatenate(
                     [total_ref[n, 6:8, :], total_ref[n, 14:16, :], total_ref[n, 22:24, :], jnp.zeros((2, LANES), F32)],
                     axis=0,
                 )
-                for far, value in enumerate((kept + from_x[n], from_y[n] + from_xy[n])):
+                for far, value in enumerate((kept + from_x[n], from_y[far_n] + from_xy[far_n])):
                     value = jnp.where(valid[p], value, 0.0)
                     first = ((y ^ far) * 2 + (core ^ side)) * (levels // 4)
                     for plane in range(planes):
@@ -197,7 +203,7 @@
     shape = jax.ShapeDtypeStruct
 
     functions = legendre.transpose(0, 2, 3, 1, 4).reshape(slots * halves * 2, sums)
-    other_functions = flipped(functions, "lev", 2)
+    other_functions = flipped(functions, "lev", 3)
 
     rows = fourier.transpose(0, 1, 2, 4, 5, 3, 6).reshape(-1, waves)
     block = shape((2 * fields * pairs, LANES), BF16)
@@ -221,10 +227,10 @@
         name="prepare",
     )(*[pltpu.with_memory_space_constraint(v, pltpu.HBM) for v in (lat_points, wave_slots.reshape(1, -1), rows, functions, vertical)])
 
-    far = tuple(reversed(range(1, bands)))
+    steps = tuple(range(1, bands))
     own = {0: blocks[0]}
-    for k in far:
-        own[k] = flipped(blocks[k], "band", k)
+    for k in steps:
+        own[k] = lax.ppermute(blocks[k], ("band", "lev"), crossed(k))
     table, weights = pl.pallas_call(
         functools.partial(spread_kernel, (planes, slots, halves, sums)),
         in_specs=[VMEM] * 3,
@@ -235,7 +241,7 @@
         name="spread",
     )(functions, other_functions, vertical)
     other = {}
-    for k in (0, *far):
+    for k in (0, *steps):
         other[k] = flipped(own[k], "lev", 1)
 
     count = 4 * fields
@@ -248,11 +254,11 @@
         scratch_shapes=[pltpu.VMEM((2 * bands, *block.shape), F32)],
         compiler_params=pltpu.CompilerParams(vmem_limit_bytes=GRANT),
         name="sum",
-    )(*[own[k] for k in range(bands)], *[other[k] for k in range(bands)], table)
-
-    from_xy = lax.ppermute(to_xy, ("lev", "grp"), [(i, i ^ 5) for i in range(8)])
+    )(own[0], *[other[k] for k in steps], other[0], *[own[k] for k in steps], table)
+
+    from_xy = lax.ppermute(to_xy, ("lev", "grp"), [(i, i ^ 7) for i in range(8)])
     from_x = flipped(to_x, "grp", 1)
-    from_y = flipped(to_y, "lev", 2)
+    from_y = flipped(to_y, "lev", 3)
     own_halves = halves // 2
     out_rows = 2 * (fields + 1) * levels * own_halves * 2
     out = pl.pallas_call(

time: 22.6 us -> 19.2 us (0.85)
  waiting for transfers between devices: 7.67 us -> 3.55 us
  starting transfers between devices: 11.5 us -> 12.3 us
    ppermute x1 -> x4, starting transfers between devices: 1.5 us -> 7.01 us  [the longest x3 5.56 us: fast_body(): own[k] = lax.ppermute(blocks[k], ('band', 'lev'), crossed(k))]
    ppermute x10 -> x7, waiting for transfers between devices: 6.43 us -> 1.4 us  [flipped(): lax.ppermute(value, axis, [(i, i ^ step) for i in range(lax.axis_size(axi...]
    ppermute x10 -> x7, starting transfers between devices: 10 us -> 5.28 us  [flipped(): lax.ppermute(value, axis, [(i, i ^ step) for i in range(lax.axis_size(axi...]
    ppermute x1 -> x4, waiting for transfers between devices: 1.24 us -> 2.16 us  [the longest x1 1.22 us: fast_body(): lax.ppermute(to_xy, ('lev', 'grp'), [(i, i ^ 7) for i in range(8)])]
  transfers between devices with their start and end apart: 11 -> 11, of which waited for: 6 -> 6; matrix products, arithmetic and copies ran while one was open for 0% -> 0% of each run, Pallas kernels for 8% -> 9%
where the time goes in v1:
time: 19.2 us; the launch traced here: 19.1 us
  starting transfers between devices  12.3 us (64%)
  waiting for transfers between devices  3.55 us (18%)
  Pallas kernels  3.17 us (17%)
    ppermute x3, starting transfers between devices, fast_body(): own[k] = lax.ppermute(blocks[k], ('band', 'lev'), crossed(k))  5.56 us
    ppermute x7, starting transfers between devices, flipped(): lax.ppermute(value, axis, [(i, i ^ step) for i in range(lax.axis_size(axi...  5.28 us
    ppermute x1, starting transfers between devices, fast_body(): lax.ppermute(to_xy, ('lev', 'grp'), [(i, i ^ 7) for i in range(8)])  1.45 us
    ppermute x7, waiting for transfers between devices, flipped(): lax.ppermute(value, axis, [(i, i ^ step) for i in range(lax.axis_size(axi...  1.4 us
    ppermute x1, waiting for transfers between devices, fast_body(): lax.ppermute(to_xy, ('lev', 'grp'), [(i, i ^ 7) for i in range(8)])  1.22 us
    pallas_call x1, Pallas kernels, fast_body(): pl.pallas_call(functools.partial(prepare_kernel, (fields, planes, pairs,...  1.16 us
    ppermute x3, waiting for transfers between devices, fast_body(): own[k] = lax.ppermute(blocks[k], ('band', 'lev'), crossed(k))  0.93 us
    pallas_call x1, Pallas kernels, fast_body(): pl.pallas_call(functools.partial(finish_kernel, (fields, levels, own_halv...  0.89 us
  transfers between devices with their start and end apart: 11, of which 6 were waited for; matrix products, arithmetic and copies ran while one was open for 0% of the time, Pallas kernels for 9%

profile of v1, /device:TPU:0, one launch (start us, length us, event | category | flops | bytes accessed | tf_op | source)
XLA Modules:
  0.0 19.1 jit_solution(14214934388231926687)
XLA Ops:
  0.0 2.4 %collective-permute-start = (bf16[576,48]{1,0:T(8,128)(2,1)}, bf16[576,48]{1,0:T(8,128)(2,1)S(1)}, u32[]{:S(2)}, u32[]{:S(2)}) collective-permute-start(bf16[576,48]{1,0:T(8,128)(2,1)} %bitcast.10), channel_id=1, source_target_pairs={{0,6},{2,4},{4,2},{6,0},{1,7},{3,5},{5,3},{7,1},{8,14},{10,12},{12... | collective-permute-start | bytes 165896 | tf_op jit(solution)/shard_map/ppermute | solution.py:16
  2.4 1.2 %prepare.1 = (s32[8,128]{1,0:T(8,128)S(1)}, bf16[576,48]{1,0:T(8,128)(2,1)S(1)}, f32[8,8]{1,0:T(8,128)S(1)}, bf16[72,128]{1,0:T(8,128)(2,1)S(1)}, bf16[72,128]{1...) custom-call(s32[1,12]{1,0:T(1,128)} %lat_hbm.1, s32[1,96]{1,0:T(1,128)} %bitcast.13, ...), custom_call_target="tpu_custom_call" | custom-call | tf_op jit(solution)/shard_map/prepare/pallas_call | solution.py:210
  3.6 1.9 %collective-permute-start.1 = (bf16[72,128]{1,0:T(8,128)(2,1)S(1)}, bf16[72,128]{1,0:T(8,128)(2,1)S(1)}, u32[]{:S(2)}, u32[]{:S(2)}) collective-permute-start(bf16[72,128]{1,0:T(8,128)(2,1)S(1)} %get-tuple-element.23), channel_id=1, source_target_pairs={{0,10},{2,8},{4,14},{6,12},{8,18},{10,16},{12,22},{14,20},{16,26},... | collective-permute-start | bytes 55304 | tf_op jit(solution)/shard_map/ppermute | solution.py:233
  5.5 2.0 %collective-permute-start.3 = (bf16[72,128]{1,0:T(8,128)(2,1)S(1)}, bf16[72,128]{1,0:T(8,128)(2,1)S(1)}, u32[]{:S(2)}, u32[]{:S(2)}) collective-permute-start(bf16[72,128]{1,0:T(8,128)(2,1)S(1)} %get-tuple-element.24), channel_id=1, source_target_pairs={{0,18},{2,16},{4,22},{6,20},{8,26},{10,24},{12,30},{14,28},{16,2},... | collective-permute-start | bytes 55304 | tf_op jit(solution)/shard_map/ppermute | solution.py:233
  7.5 1.6 %collective-permute-start.5 = (bf16[72,128]{1,0:T(8,128)(2,1)S(1)}, bf16[72,128]{1,0:T(8,128)(2,1)S(1)}, u32[]{:S(2)}, u32[]{:S(2)}) collective-permute-start(bf16[72,128]{1,0:T(8,128)(2,1)S(1)} %get-tuple-element.25), channel_id=1, source_target_pairs={{0,26},{2,24},{4,30},{6,28},{8,2},{10,0},{12,6},{14,4},{16,10},{18... | collective-permute-start | bytes 55304 | tf_op jit(solution)/shard_map/ppermute | solution.py:233
  9.2 0.0 collective-permute-start.7
  9.2 0.0 collective-permute-done.1.refs_5_
  9.2 0.5 %collective-permute-start.2 = (bf16[72,128]{1,0:T(8,128)(2,1)S(1)}, bf16[72,128]{1,0:T(8,128)(2,1)S(1)}, u32[]{:S(2)}, u32[]{:S(2)}) collective-permute-start(bf16[72,128]{1,0:T(8,128)(2,1)S(1)} %collective-permute-done.1.refs_5_), channel_id=1, source_target_pairs={{0,2},{2,0},{4,6},{6,4},{1,3},{3,1},{5,7},{7,5},{8,10},{10,8},{12,... | collective-permute-start | bytes 55304 | tf_op jit(solution)/shard_map/ppermute | solution.py:16
  9.7 0.1 collective-permute-done.3.refs_6_
  9.7 0.1 collective-permute-start.4
  9.9 0.9 %collective-permute-done.5.refs_7_ = bf16[72,128]{1,0:T(8,128)(2,1)S(1)} collective-permute-done((bf16[72,128]{1,0:T(8,128)(2,1)S(1)}, bf16[72,128]{1,0:T(8,128)(2,1)S(1)}, u32[]{:S(2)}, u32[]{:S(2)}) %collective-permute-start.5) | collective-permute-done | bytes 18464 | tf_op jit(solution)/shard_map/ppermute | solution.py:233
  10.7 0.7 %collective-permute-start.6 = (bf16[72,128]{1,0:T(8,128)(2,1)S(1)}, bf16[72,128]{1,0:T(8,128)(2,1)S(1)}, u32[]{:S(2)}, u32[]{:S(2)}) collective-permute-start(bf16[72,128]{1,0:T(8,128)(2,1)S(1)} %collective-permute-done.5.refs_7_), channel_id=1, source_target_pairs={{0,2},{2,0},{4,6},{6,4},{1,3},{3,1},{5,7},{7,5},{8,10},{10,8},{12,... | collective-permute-start | bytes 55304 | tf_op jit(solution)/shard_map/ppermute | solution.py:16
  11.4 0.0 collective-permute-done.other_ref
  11.4 0.6 %spread.1 = (f32[2,1152,128]{2,1,0:T(8,128)S(1)}, f32[64,8,128]{2,1,0:T(8,128)S(1)}) custom-call(bf16[576,48]{1,0:T(8,128)(2,1)S(1)} %get-tuple-element.18.own_ref, bf16[576,48]{1,0:T(8,128)(2,1)S(1)} %collective-permute-done.other_ref, f32[8,8]{1,0:T(8,128)S(1)} %get-tuple-element.19.vertical_ref), custom_call_target="tpu_custom_call" | custom-call | tf_op jit(solution)/shard_map/spread/pallas_call | solution.py:234
  12.0 0.0 collective-permute-done.7.refs_4_
  12.0 0.0 collective-permute-done.2.refs_1_
  12.1 0.0 collective-permute-done.4.refs_2_
  12.1 0.2 collective-permute-done.6.refs_3_
  12.2 0.5 %sum.1 = (f32[12,24,128]{2,1,0:T(8,128)S(1)}, bf16[96,128]{1,0:T(8,128)(2,1)S(1)}, bf16[96,128]{1,0:T(8,128)(2,1)S(1)}, bf16[96,128]{1,0:T(8,128)(2,1)S(1)}) custom-call(bf16[72,128]{1,0:T(8,128)(2,1)S(1)} %get-tuple-element.22.refs_0_, bf16[72,128]{1,0:T(8,128)(2,1)S(1)} %collective-permute-done.2.refs_1_, ...), custom_call_target="tpu_custom_call" | custom-call | tf_op jit(solution)/shard_map/sum/pallas_call | solution.py:249
  12.8 1.4 %collective-permute-start.10 = (bf16[96,128]{1,0:T(8,128)(2,1)S(1)}, bf16[96,128]{1,0:T(8,128)(2,1)S(1)}, u32[]{:S(2)}, u32[]{:S(2)}) collective-permute-start(bf16[96,128]{1,0:T(8,128)(2,1)S(1)} %get-tuple-element.30), channel_id=1, source_target_pairs={{0,7},{1,6},{2,5},{3,4},{4,3},{5,2},{6,1},{7,0},{8,15},{9,14},{10,... | collective-permute-start | bytes 73736 | tf_op jit(solution)/shard_map/ppermute | solution.py:259
  14.2 0.5 %collective-permute-start.8 = (bf16[96,128]{1,0:T(8,128)(2,1)S(1)}, bf16[96,128]{1,0:T(8,128)(2,1)S(1)}, u32[]{:S(2)}, u32[]{:S(2)}) collective-permute-start(bf16[96,128]{1,0:T(8,128)(2,1)S(1)} %get-tuple-element.28), channel_id=1, source_target_pairs={{0,1},{1,0},{2,3},{3,2},{4,5},{5,4},{6,7},{7,6},{8,9},{9,8},{10,11... | collective-permute-start | bytes 73736 | tf_op jit(solution)/shard_map/ppermute | solution.py:16
  14.7 1.0 %collective-permute-start.9 = (bf16[96,128]{1,0:T(8,128)(2,1)S(1)}, bf16[96,128]{1,0:T(8,128)(2,1)S(1)}, u32[]{:S(2)}, u32[]{:S(2)}) collective-permute-start(bf16[96,128]{1,0:T(8,128)(2,1)S(1)} %get-tuple-element.29), channel_id=1, source_target_pairs={{0,6},{2,4},{4,2},{6,0},{1,7},{3,5},{5,3},{7,1},{8,14},{10,12},{12... | collective-permute-start | bytes 73736 | tf_op jit(solution)/shard_map/ppermute | solution.py:16
  15.8 1.2 %collective-permute-done.10.xy_ref = bf16[96,128]{1,0:T(8,128)(2,1)S(1)} collective-permute-done((bf16[96,128]{1,0:T(8,128)(2,1)S(1)}, bf16[96,128]{1,0:T(8,128)(2,1)S(1)}, u32[]{:S(2)}, u32[]{:S(2)}) %collective-permute-start.10) | collective-permute-done | bytes 24608 | tf_op jit(solution)/shard_map/ppermute | solution.py:259
  17.0 1.1 %collective-permute-done.8.x_ref = bf16[96,128]{1,0:T(8,128)(2,1)S(1)} collective-permute-done((bf16[96,128]{1,0:T(8,128)(2,1)S(1)}, bf16[96,128]{1,0:T(8,128)(2,1)S(1)}, u32[]{:S(2)}, u32[]{:S(2)}) %collective-permute-start.8) | collective-permute-done | bytes 24608 | tf_op jit(solution)/shard_map/ppermute | solution.py:16
  18.0 0.1 collective-permute-done.9.y_ref
  18.2 0.9 %finish.1 = bf16[768,24]{1,0:T(8,128)(2,1)} custom-call(f32[64,8,128]{2,1,0:T(8,128)S(1)} %get-tuple-element.20.weights_ref, s32[8,128]{1,0:T(8,128)S(1)} %get-tuple-element.21.slot_lanes_ref, f32[12,24,128]{2,1,0:T(8,128)S(1)} %get-tuple-element.27.total_ref, bf16[96,128]{1,0:T(8,128)(2,1)S(1)} %collective-permute-done.8.x_ref, ...), custom_call_target="tpu_custom_call" | custom-call | tf_op jit(solution)/shard_map/finish/pallas_call | solution.py:264
Async XLA Ops:
  0.0 11.4 %collective-permute-start = (bf16[576,48]{1,0:T(8,128)(2,1)}, bf16[576,48]{1,0:T(8,128)(2,1)S(1)}, u32[]{:S(2)}, u32[]{:S(2)}) collective-permute-start(bf16[576,48]{1,0:T(8,128)(2,1)} %bitcast.10), channel_id=1, source_target_pairs={{0,6},{2,4},{4,2},{6,0},{1,7},{3,5},{5,3},{7,1},{8,14},{10,12},{12... | collective-permute-start | bytes 165896 | tf_op jit(solution)/shard_map/ppermute | solution.py:16
  3.6 5.6 %collective-permute-start.1 = (bf16[72,128]{1,0:T(8,128)(2,1)S(1)}, bf16[72,128]{1,0:T(8,128)(2,1)S(1)}, u32[]{:S(2)}, u32[]{:S(2)}) collective-permute-start(bf16[72,128]{1,0:T(8,128)(2,1)S(1)} %get-tuple-element.23), channel_id=1, source_target_pairs={{0,10},{2,8},{4,14},{6,12},{8,18},{10,16},{12,22},{14,20},{16,26},... | collective-permute-start | bytes 55304 | tf_op jit(solution)/shard_map/ppermute | solution.py:233
  5.5 4.2 %collective-permute-start.3 = (bf16[72,128]{1,0:T(8,128)(2,1)S(1)}, bf16[72,128]{1,0:T(8,128)(2,1)S(1)}, u32[]{:S(2)}, u32[]{:S(2)}) collective-permute-start(bf16[72,128]{1,0:T(8,128)(2,1)S(1)} %get-tuple-element.24), channel_id=1, source_target_pairs={{0,18},{2,16},{4,22},{6,20},{8,26},{10,24},{12,30},{14,28},{16,2},... | collective-permute-start | bytes 55304 | tf_op jit(solution)/shard_map/ppermute | solution.py:233
  7.5 3.2 %collective-permute-start.5 = (bf16[72,128]{1,0:T(8,128)(2,1)S(1)}, bf16[72,128]{1,0:T(8,128)(2,1)S(1)}, u32[]{:S(2)}, u32[]{:S(2)}) collective-permute-start(bf16[72,128]{1,0:T(8,128)(2,1)S(1)} %get-tuple-element.25), channel_id=1, source_target_pairs={{0,26},{2,24},{4,30},{6,28},{8,2},{10,0},{12,6},{14,4},{16,10},{18... | collective-permute-start | bytes 55304 | tf_op jit(solution)/shard_map/ppermute | solution.py:233
  9.2 2.9 %collective-permute-start.7 = (bf16[72,128]{1,0:T(8,128)(2,1)S(1)}, bf16[72,128]{1,0:T(8,128)(2,1)S(1)}, u32[]{:S(2)}, u32[]{:S(2)}) collective-permute-start(bf16[72,128]{1,0:T(8,128)(2,1)S(1)} %get-tuple-element.22.refs_0_), channel_id=1, source_target_pairs={{0,2},{2,0},{4,6},{6,4},{1,3},{3,1},{5,7},{7,5},{8,10},{10,8},{12,... | collective-permute-start | bytes 55304 | tf_op jit(solution)/shard_map/ppermute | solution.py:16
  9.2 2.9 %collective-permute-start.2 = (bf16[72,128]{1,0:T(8,128)(2,1)S(1)}, bf16[72,128]{1,0:T(8,128)(2,1)S(1)}, u32[]{:S(2)}, u32[]{:S(2)}) collective-permute-start(bf16[72,128]{1,0:T(8,128)(2,1)S(1)} %collective-permute-done.1.refs_5_), channel_id=1, source_target_pairs={{0,2},{2,0},{4,6},{6,4},{1,3},{3,1},{5,7},{7,5},{8,10},{10,8},{12,... | collective-permute-start | bytes 55304 | tf_op jit(solution)/shard_map/ppermute | solution.py:16
  9.7 2.3 %collective-permute-start.4 = (bf16[72,128]{1,0:T(8,128)(2,1)S(1)}, bf16[72,128]{1,0:T(8,128)(2,1)S(1)}, u32[]{:S(2)}, u32[]{:S(2)}) collective-permute-start(bf16[72,128]{1,0:T(8,128)(2,1)S(1)} %collective-permute-done.3.refs_6_), channel_id=1, source_target_pairs={{0,2},{2,0},{4,6},{6,4},{1,3},{3,1},{5,7},{7,5},{8,10},{10,8},{12,... | collective-permute-start | bytes 55304 | tf_op jit(solution)/shard_map/ppermute | solution.py:16
  10.7 1.5 %collective-permute-start.6 = (bf16[72,128]{1,0:T(8,128)(2,1)S(1)}, bf16[72,128]{1,0:T(8,128)(2,1)S(1)}, u32[]{:S(2)}, u32[]{:S(2)}) collective-permute-start(bf16[72,128]{1,0:T(8,128)(2,1)S(1)} %collective-permute-done.5.refs_7_), channel_id=1, source_target_pairs={{0,2},{2,0},{4,6},{6,4},{1,3},{3,1},{5,7},{7,5},{8,10},{10,8},{12,... | collective-permute-start | bytes 55304 | tf_op jit(solution)/shard_map/ppermute | solution.py:16
  12.8 4.2 %collective-permute-start.10 = (bf16[96,128]{1,0:T(8,128)(2,1)S(1)}, bf16[96,128]{1,0:T(8,128)(2,1)S(1)}, u32[]{:S(2)}, u32[]{:S(2)}) collective-permute-start(bf16[96,128]{1,0:T(8,128)(2,1)S(1)} %get-tuple-element.30), channel_id=1, source_target_pairs={{0,7},{1,6},{2,5},{3,4},{4,3},{5,2},{6,1},{7,0},{8,15},{9,14},{10,... | collective-permute-start | bytes 73736 | tf_op jit(solution)/shard_map/ppermute | solution.py:259
  14.2 3.8 %collective-permute-start.8 = (bf16[96,128]{1,0:T(8,128)(2,1)S(1)}, bf16[96,128]{1,0:T(8,128)(2,1)S(1)}, u32[]{:S(2)}, u32[]{:S(2)}) collective-permute-start(bf16[96,128]{1,0:T(8,128)(2,1)S(1)} %get-tuple-element.28), channel_id=1, source_target_pairs={{0,1},{1,0},{2,3},{3,2},{4,5},{5,4},{6,7},{7,6},{8,9},{9,8},{10,11... | collective-permute-start | bytes 73736 | tf_op jit(solution)/shard_map/ppermute | solution.py:16
  14.7 3.4 %collective-permute-start.9 = (bf16[96,128]{1,0:T(8,128)(2,1)S(1)}, bf16[96,128]{1,0:T(8,128)(2,1)S(1)}, u32[]{:S(2)}, u32[]{:S(2)}) collective-permute-start(bf16[96,128]{1,0:T(8,128)(2,1)S(1)} %get-tuple-element.29), channel_id=1, source_target_pairs={{0,6},{2,4},{4,2},{6,0},{1,7},{3,5},{5,3},{7,1},{8,14},{10,12},{12... | collective-permute-start | bytes 73736 | tf_op jit(solution)/shard_map/ppermute | solution.py:16

commit v2 on v1

--- a/solution.py
+++ b/solution.py
@@ -16,9 +16,31 @@
     return lax.ppermute(value, axis, [(i, i ^ step) for i in range(lax.axis_size(axis))])
 
 
-def crossed(step):
+def rounds(bands):
+    if bands == 4:
+        return ((2, 3, 1, 0), (3, 2, 0, 1), (1, 0, 3, 2))
+    return tuple(tuple((b + k) % bands for b in range(bands)) for k in range(1, bands))
+
+
+def picked(table, index):
+    value = jnp.int32(table[0])
+    for i in range(1, len(table)):
+        value = jnp.where(index == i, table[i], value)
+    return value
+
+
+def target(bands, band, k):
+    return picked(rounds(bands)[k - 1], band) if k else band
+
+
+def source(bands, band, k):
+    return picked([rounds(bands)[k - 1].index(b) for b in range(bands)], band) if k else band
+
+
+def crossed(k):
     bands, levs = lax.axis_size("band"), lax.axis_size("lev")
-    return [(b * levs + v, (b + step) % bands * levs + (v ^ 1)) for b in range(bands) for v in range(levs)]
+    to = rounds(bands)[k - 1]
+    return [(b * levs + v, to[b] * levs + (v ^ 1)) for b in range(bands) for v in range(levs)]
 
 
 def iota(shape, dim):
@@ -31,8 +53,8 @@
     width = LANES // planes
     band = lax.axis_index("band")
     copies = [
-        pltpu.make_async_copy(source, target, sems.at[i])
-        for i, (source, target) in enumerate(
+        pltpu.make_async_copy(given, held, sems.at[i])
+        for i, (given, held) in enumerate(
             (
                 (slots_hbm, slots_ref),
                 (lat_hbm, lat_ref),
@@ -48,7 +70,7 @@
     copies[0].wait()
     tables = []
     for k in range(len(block_refs)):
-        first = lax.rem(band + k, len(block_refs)) * slots
+        first = target(len(block_refs), band, k) * slots
         held = jnp.full((8, LANES), -1, jnp.int32)
         for s in range(slots):
             held = jnp.where(lane % width == s, slots_ref[0, first + s], held)
@@ -123,23 +145,36 @@
                     out_ref[p, pl.ds(start, sums, stride=24), :] = copies
 
 
-def sum_kernel(dims, *refs):
+def add_products(dims, parts, table_ref, rows_ref, p, totals):
     fields, pairs, bands = dims
-    blocks, (table_ref, total_ref, x_ref, y_ref, xy_ref, rows_ref) = refs[: 2 * bands], refs[2 * bands :]
     band = lax.axis_index("band")
-    for i, block in enumerate(blocks):
-        rows_ref[i] = block[...].astype(F32)
+    for i, (side, k) in enumerate(parts):
+        first = source(bands, band, k) * pairs
+        for q in range(pairs):
+            factors = table_ref[p, pl.ds(pl.multiple_of((first + q) * 24, 8), 24), :]
+            for f in range(fields):
+                row = (f * pairs + q) * 2 + p
+                totals[side * fields + f] += rows_ref[i, row : row + 1, :] * factors
+
+
+def sum_first_kernel(dims, parts, *refs):
+    block_refs, (table_ref, total_ref, rows_ref) = refs[:-3], refs[-3:]
+    for i, block_ref in enumerate(block_refs):
+        rows_ref[i] = block_ref[...].astype(F32)
     for p in range(2):
-        totals = [jnp.zeros((24, LANES), F32) for _ in range(2 * fields)]
-        for k in range(bands):
-            first = lax.rem(band + bands - k, bands) * pairs
-            for q in range(pairs):
-                factors = table_ref[p, pl.ds(pl.multiple_of((first + q) * 24, 8), 24), :]
-                for side in range(2):
-                    for f in range(fields):
-                        row = (f * pairs + q) * 2 + p
-                        i = side * fields + f
-                        totals[i] += rows_ref[side * bands + k, row : row + 1, :] * factors
+        totals = [jnp.zeros((24, LANES), F32) for _ in range(2 * dims[0])]
+        add_products(dims, parts, table_ref, rows_ref, p, totals)
+        for i, total in enumerate(totals):
+            total_ref[2 * i + p] = total
+
+
+def sum_kernel(dims, parts, *refs):
+    block_refs, (table_ref, before_ref, total_ref, x_ref, y_ref, xy_ref, rows_ref) = refs[:-7], refs[-7:]
+    for i, block_ref in enumerate(block_refs):
+        rows_ref[i] = block_ref[...].astype(F32)
+    for p in range(2):
+        totals = [before_ref[2 * i + p] for i in range(2 * dims[0])]
+        add_products(dims, parts, table_ref, rows_ref, p, totals)
         for i, total in enumerate(totals):
             total_ref[2 * i + p] = total
     for at, ref in ((0, x_ref), (8, y_ref), (16, xy_ref)):
@@ -246,15 +281,26 @@
 
     count = 4 * fields
     message = shape((count * 8, LANES), BF16)
+    totals = shape((count, 24, LANES), F32)
+    direct = [(0, 0), *[(1, k) for k in steps]]
+    before = pl.pallas_call(
+        functools.partial(sum_first_kernel, (fields, pairs, bands), direct),
+        in_specs=[VMEM] * (bands + 1),
+        out_specs=VMEM,
+        out_shape=totals,
+        scratch_shapes=[pltpu.VMEM((bands, *block.shape), F32)],
+        compiler_params=pltpu.CompilerParams(vmem_limit_bytes=GRANT),
+        name="sum_first",
+    )(*[own[k] for k in range(bands)], table)
     total, to_x, to_y, to_xy = pl.pallas_call(
-        functools.partial(sum_kernel, (fields, pairs, bands)),
-        in_specs=[VMEM] * (2 * bands + 1),
+        functools.partial(sum_kernel, (fields, pairs, bands), [(1 - side, k) for side, k in direct]),
+        in_specs=[VMEM] * (bands + 2),
         out_specs=[VMEM] * 4,
-        out_shape=[shape((count, 24, LANES), F32)] + [message] * 3,
-        scratch_shapes=[pltpu.VMEM((2 * bands, *block.shape), F32)],
+        out_shape=[totals] + [message] * 3,
+        scratch_shapes=[pltpu.VMEM((bands, *block.shape), F32)],
         compiler_params=pltpu.CompilerParams(vmem_limit_bytes=GRANT),
         name="sum",
-    )(own[0], *[other[k] for k in steps], other[0], *[own[k] for k in steps], table)
+    )(*[other[k] for k in range(bands)], table, before)
 
     from_xy = lax.ppermute(to_xy, ("lev", "grp"), [(i, i ^ 7) for i in range(8)])
     from_x = flipped(to_x, "grp", 1)

time: 19.2 us -> 19.3 us (level)
  waiting for transfers between devices: 3.55 us -> 4.82 us
  starting transfers between devices: 12.3 us -> 11.1 us
    ppermute x3, starting transfers between devices: 5.56 us -> 4 us  [fast_body(): own[k] = lax.ppermute(blocks[k], ('band', 'lev'), crossed(k))]
    ppermute x3, waiting for transfers between devices: 0.93 us -> 2.35 us  [fast_body(): own[k] = lax.ppermute(blocks[k], ('band', 'lev'), crossed(k))]
    ppermute x1, waiting for transfers between devices: 1.22 us -> 0.81 us  [fast_body(): lax.ppermute(to_xy, ('lev', 'grp'), [(i, i ^ 7) for i in range(8)])]
    ppermute x7, waiting for transfers between devices: 1.4 us -> 1.67 us  [flipped(): lax.ppermute(value, axis, [(i, i ^ step) for i in range(lax.axis_size(axi...]
    ppermute x1, starting transfers between devices: 1.45 us -> 1.69 us  [fast_body(): lax.ppermute(to_xy, ('lev', 'grp'), [(i, i ^ 7) for i in range(8)])]
    pallas_call x1 -> x2, Pallas kernels: 0.51 us -> 0.54 us  [the longest x1 0.28 us: fast_body(): pl.pallas_call(functools.partial(sum_kernel, (fields, pairs, bands), [(1...]
  transfers between devices with their start and end apart: 11 -> 11, of which waited for: 6 -> 6; matrix products, arithmetic and copies ran while one was open for 0% -> 0% of each run, Pallas kernels for 9% -> 11%
where the time goes in v2:
time: 19.3 us; the launch traced here: 19.2 us
  starting transfers between devices  11.1 us (58%)
  waiting for transfers between devices  4.82 us (25%)
  Pallas kernels  3.21 us (17%)
    ppermute x7, starting transfers between devices, flipped(): lax.ppermute(value, axis, [(i, i ^ step) for i in range(lax.axis_size(axi...  5.38 us
    ppermute x3, starting transfers between devices, fast_body(): own[k] = lax.ppermute(blocks[k], ('band', 'lev'), crossed(k))  4 us
    ppermute x3, waiting for transfers between devices, fast_body(): own[k] = lax.ppermute(blocks[k], ('band', 'lev'), crossed(k))  2.35 us
    ppermute x1, starting transfers between devices, fast_body(): lax.ppermute(to_xy, ('lev', 'grp'), [(i, i ^ 7) for i in range(8)])  1.69 us
    ppermute x7, waiting for transfers between devices, flipped(): lax.ppermute(value, axis, [(i, i ^ step) for i in range(lax.axis_size(axi...  1.67 us
    pallas_call x1, Pallas kernels, fast_body(): pl.pallas_call(functools.partial(prepare_kernel, (fields, planes, pairs,...  1.16 us
    pallas_call x1, Pallas kernels, fast_body(): pl.pallas_call(functools.partial(finish_kernel, (fields, levels, own_halv...  0.89 us
    ppermute x1, waiting for transfers between devices, fast_body(): lax.ppermute(to_xy, ('lev', 'grp'), [(i, i ^ 7) for i in range(8)])  0.81 us
  transfers between devices with their start and end apart: 11, of which 6 were waited for; matrix products, arithmetic and copies ran while one was open for 0% of the time, Pallas kernels for 11%

profile of v2, /device:TPU:0, one launch (start us, length us, event | category | flops | bytes accessed | tf_op | source)
XLA Modules:
  0.0 19.2 jit_solution(12127722717263510639)
XLA Ops:
  0.0 2.4 %collective-permute-start = (bf16[576,48]{1,0:T(8,128)(2,1)}, bf16[576,48]{1,0:T(8,128)(2,1)S(1)}, u32[]{:S(2)}, u32[]{:S(2)}) collective-permute-start(bf16[576,48]{1,0:T(8,128)(2,1)} %bitcast.10), channel_id=1, source_target_pairs={{0,6},{2,4},{4,2},{6,0},{1,7},{3,5},{5,3},{7,1},{8,14},{10,12},{12... | collective-permute-start | bytes 165896 | tf_op jit(solution)/shard_map/ppermute | solution.py:16
  2.4 1.2 %prepare.1 = (s32[8,128]{1,0:T(8,128)S(1)}, bf16[576,48]{1,0:T(8,128)(2,1)S(1)}, f32[8,8]{1,0:T(8,128)S(1)}, bf16[72,128]{1,0:T(8,128)(2,1)S(1)}, bf16[72,128]{1...) custom-call(s32[1,12]{1,0:T(1,128)} %lat_hbm.1, s32[1,96]{1,0:T(1,128)} %bitcast.13, ...), custom_call_target="tpu_custom_call" | custom-call | tf_op jit(solution)/shard_map/prepare/pallas_call | solution.py:245
  3.6 2.9 %collective-permute-start.2 = (bf16[72,128]{1,0:T(8,128)(2,1)S(1)}, bf16[72,128]{1,0:T(8,128)(2,1)S(1)}, u32[]{:S(2)}, u32[]{:S(2)}) collective-permute-start(bf16[72,128]{1,0:T(8,128)(2,1)S(1)} %get-tuple-element.23), channel_id=1, source_target_pairs={{0,18},{2,16},{4,22},{6,20},{8,26},{10,24},{12,30},{14,28},{16,10}... | collective-permute-start | bytes 55304 | tf_op jit(solution)/shard_map/ppermute | solution.py:268
  6.5 1.1 %collective-permute-start.4 = (bf16[72,128]{1,0:T(8,128)(2,1)S(1)}, bf16[72,128]{1,0:T(8,128)(2,1)S(1)}, u32[]{:S(2)}, u32[]{:S(2)}) collective-permute-start(bf16[72,128]{1,0:T(8,128)(2,1)S(1)} %get-tuple-element.24), channel_id=1, source_target_pairs={{0,26},{2,24},{4,30},{6,28},{8,18},{10,16},{12,22},{14,20},{16,2},... | collective-permute-start | bytes 55304 | tf_op jit(solution)/shard_map/ppermute | solution.py:268
  7.6 0.0 collective-permute-start.6
  7.6 0.6 %collective-permute-start.1 = (bf16[72,128]{1,0:T(8,128)(2,1)S(1)}, bf16[72,128]{1,0:T(8,128)(2,1)S(1)}, u32[]{:S(2)}, u32[]{:S(2)}) collective-permute-start(bf16[72,128]{1,0:T(8,128)(2,1)S(1)} %get-tuple-element.22.refs_0_), channel_id=1, source_target_pairs={{0,2},{2,0},{4,6},{6,4},{1,3},{3,1},{5,7},{7,5},{8,10},{10,8},{12,... | collective-permute-start | bytes 55304 | tf_op jit(solution)/shard_map/ppermute | solution.py:16
  8.2 0.8 %collective-permute-done.2.refs_1_ = bf16[72,128]{1,0:T(8,128)(2,1)S(1)} collective-permute-done((bf16[72,128]{1,0:T(8,128)(2,1)S(1)}, bf16[72,128]{1,0:T(8,128)(2,1)S(1)}, u32[]{:S(2)}, u32[]{:S(2)}) %collective-permute-start.2) | collective-permute-done | bytes 18464 | tf_op jit(solution)/shard_map/ppermute | solution.py:268
  9.0 0.3 %collective-permute-start.3 = (bf16[72,128]{1,0:T(8,128)(2,1)S(1)}, bf16[72,128]{1,0:T(8,128)(2,1)S(1)}, u32[]{:S(2)}, u32[]{:S(2)}) collective-permute-start(bf16[72,128]{1,0:T(8,128)(2,1)S(1)} %collective-permute-done.2.refs_1_), channel_id=1, source_target_pairs={{0,2},{2,0},{4,6},{6,4},{1,3},{3,1},{5,7},{7,5},{8,10},{10,8},{12,... | collective-permute-start | bytes 55304 | tf_op jit(solution)/shard_map/ppermute | solution.py:16
  9.3 1.5 %collective-permute-done.4.refs_2_ = bf16[72,128]{1,0:T(8,128)(2,1)S(1)} collective-permute-done((bf16[72,128]{1,0:T(8,128)(2,1)S(1)}, bf16[72,128]{1,0:T(8,128)(2,1)S(1)}, u32[]{:S(2)}, u32[]{:S(2)}) %collective-permute-start.4) | collective-permute-done | bytes 18464 | tf_op jit(solution)/shard_map/ppermute | solution.py:268
  10.8 0.1 collective-permute-start.5
  10.9 0.1 collective-permute-done.6.refs_3_
  11.0 0.3 %collective-permute-start.7 = (bf16[72,128]{1,0:T(8,128)(2,1)S(1)}, bf16[72,128]{1,0:T(8,128)(2,1)S(1)}, u32[]{:S(2)}, u32[]{:S(2)}) collective-permute-start(bf16[72,128]{1,0:T(8,128)(2,1)S(1)} %collective-permute-done.6.refs_3_), channel_id=1, source_target_pairs={{0,2},{2,0},{4,6},{6,4},{1,3},{3,1},{5,7},{7,5},{8,10},{10,8},{12,... | collective-permute-start | bytes 55304 | tf_op jit(solution)/shard_map/ppermute | solution.py:16
  11.3 0.0 collective-permute-done.other_ref
  11.3 0.6 %spread.1 = (f32[2,1152,128]{2,1,0:T(8,128)S(1)}, f32[64,8,128]{2,1,0:T(8,128)S(1)}) custom-call(bf16[576,48]{1,0:T(8,128)(2,1)S(1)} %get-tuple-element.18.own_ref, bf16[576,48]{1,0:T(8,128)(2,1)S(1)} %collective-permute-done.other_ref, f32[8,8]{1,0:T(8,128)S(1)} %get-tuple-element.19.vertical_ref), custom_call_target="tpu_custom_call" | custom-call | tf_op jit(solution)/shard_map/spread/pallas_call | solution.py:269
  11.9 0.3 %sum_first.1.refs_5_ = f32[12,24,128]{2,1,0:T(8,128)S(1)} custom-call(bf16[72,128]{1,0:T(8,128)(2,1)S(1)} %get-tuple-element.22.refs_0_, bf16[72,128]{1,0:T(8,128)(2,1)S(1)} %collective-permute-done.2.refs_1_, bf16[72,128]{1,0:T(8,128)(2,1)S(1)} %collective-permute-done.4.refs_2_, bf16[72,128]{1,0:T(8,128)(2,1)S(1)} %collective-permute-done.6.refs_3_, ...), custom_call_target="tpu_custom_call" | custom-call | tf_op jit(solution)/shard_map/sum_first/pallas_call | solution.py:286
  12.2 0.0 collective-permute-done.1.refs_0_
  12.2 0.0 collective-permute-done.3.refs_1_
  12.2 0.0 collective-permute-done.5.refs_2_
  12.2 0.0 collective-permute-done.7.refs_3_
  12.2 0.3 %sum.1 = (f32[12,24,128]{2,1,0:T(8,128)S(1)}, bf16[96,128]{1,0:T(8,128)(2,1)S(1)}, bf16[96,128]{1,0:T(8,128)(2,1)S(1)}, bf16[96,128]{1,0:T(8,128)(2,1)S(1)}) custom-call(bf16[72,128]{1,0:T(8,128)(2,1)S(1)} %collective-permute-done.1.refs_0_, bf16[72,128]{1,0:T(8,128)(2,1)S(1)} %collective-permute-done.3.refs_1_, ...), custom_call_target="tpu_custom_call" | custom-call | tf_op jit(solution)/shard_map/sum/pallas_call | solution.py:295
  12.5 1.6 %collective-permute-start.8 = (bf16[96,128]{1,0:T(8,128)(2,1)S(1)}, bf16[96,128]{1,0:T(8,128)(2,1)S(1)}, u32[]{:S(2)}, u32[]{:S(2)}) collective-permute-start(bf16[96,128]{1,0:T(8,128)(2,1)S(1)} %get-tuple-element.28), channel_id=1, source_target_pairs={{0,1},{1,0},{2,3},{3,2},{4,5},{5,4},{6,7},{7,6},{8,9},{9,8},{10,11... | collective-permute-start | bytes 73736 | tf_op jit(solution)/shard_map/ppermute | solution.py:16
  14.1 0.0 collective-permute-start.9
  14.1 1.7 %collective-permute-start.10 = (bf16[96,128]{1,0:T(8,128)(2,1)S(1)}, bf16[96,128]{1,0:T(8,128)(2,1)S(1)}, u32[]{:S(2)}, u32[]{:S(2)}) collective-permute-start(bf16[96,128]{1,0:T(8,128)(2,1)S(1)} %get-tuple-element.30), channel_id=1, source_target_pairs={{0,7},{1,6},{2,5},{3,4},{4,3},{5,2},{6,1},{7,0},{8,15},{9,14},{10,... | collective-permute-start | bytes 73736 | tf_op jit(solution)/shard_map/ppermute | solution.py:305
  15.8 0.6 %collective-permute-done.8.x_ref = bf16[96,128]{1,0:T(8,128)(2,1)S(1)} collective-permute-done((bf16[96,128]{1,0:T(8,128)(2,1)S(1)}, bf16[96,128]{1,0:T(8,128)(2,1)S(1)}, u32[]{:S(2)}, u32[]{:S(2)}) %collective-permute-start.8) | collective-permute-done | bytes 24608 | tf_op jit(solution)/shard_map/ppermute | solution.py:16
  16.4 1.0 %collective-permute-done.9.y_ref = bf16[96,128]{1,0:T(8,128)(2,1)S(1)} collective-permute-done((bf16[96,128]{1,0:T(8,128)(2,1)S(1)}, bf16[96,128]{1,0:T(8,128)(2,1)S(1)}, u32[]{:S(2)}, u32[]{:S(2)}) %collective-permute-start.9) | collective-permute-done | bytes 24608 | tf_op jit(solution)/shard_map/ppermute | solution.py:16
  17.5 0.8 %collective-permute-done.10.xy_ref = bf16[96,128]{1,0:T(8,128)(2,1)S(1)} collective-permute-done((bf16[96,128]{1,0:T(8,128)(2,1)S(1)}, bf16[96,128]{1,0:T(8,128)(2,1)S(1)}, u32[]{:S(2)}, u32[]{:S(2)}) %collective-permute-start.10) | collective-permute-done | bytes 24608 | tf_op jit(solution)/shard_map/ppermute | solution.py:305
  18.3 0.9 %finish.1 = bf16[768,24]{1,0:T(8,128)(2,1)} custom-call(f32[64,8,128]{2,1,0:T(8,128)S(1)} %get-tuple-element.20.weights_ref, s32[8,128]{1,0:T(8,128)S(1)} %get-tuple-element.21.slot_lanes_ref, f32[12,24,128]{2,1,0:T(8,128)S(1)} %get-tuple-element.27.total_ref, bf16[96,128]{1,0:T(8,128)(2,1)S(1)} %collective-permute-done.8.x_ref, ...), custom_call_target="tpu_custom_call" | custom-call | tf_op jit(solution)/shard_map/finish/pallas_call | solution.py:310
Async XLA Ops:
  0.0 11.3 %collective-permute-start = (bf16[576,48]{1,0:T(8,128)(2,1)}, bf16[576,48]{1,0:T(8,128)(2,1)S(1)}, u32[]{:S(2)}, u32[]{:S(2)}) collective-permute-start(bf16[576,48]{1,0:T(8,128)(2,1)} %bitcast.10), channel_id=1, source_target_pairs={{0,6},{2,4},{4,2},{6,0},{1,7},{3,5},{5,3},{7,1},{8,14},{10,12},{12... | collective-permute-start | bytes 165896 | tf_op jit(solution)/shard_map/ppermute | solution.py:16
  3.6 5.4 %collective-permute-start.2 = (bf16[72,128]{1,0:T(8,128)(2,1)S(1)}, bf16[72,128]{1,0:T(8,128)(2,1)S(1)}, u32[]{:S(2)}, u32[]{:S(2)}) collective-permute-start(bf16[72,128]{1,0:T(8,128)(2,1)S(1)} %get-tuple-element.23), channel_id=1, source_target_pairs={{0,18},{2,16},{4,22},{6,20},{8,26},{10,24},{12,30},{14,28},{16,10}... | collective-permute-start | bytes 55304 | tf_op jit(solution)/shard_map/ppermute | solution.py:268
  6.5 4.3 %collective-permute-start.4 = (bf16[72,128]{1,0:T(8,128)(2,1)S(1)}, bf16[72,128]{1,0:T(8,128)(2,1)S(1)}, u32[]{:S(2)}, u32[]{:S(2)}) collective-permute-start(bf16[72,128]{1,0:T(8,128)(2,1)S(1)} %get-tuple-element.24), channel_id=1, source_target_pairs={{0,26},{2,24},{4,30},{6,28},{8,18},{10,16},{12,22},{14,20},{16,2},... | collective-permute-start | bytes 55304 | tf_op jit(solution)/shard_map/ppermute | solution.py:268
  7.6 3.4 %collective-permute-start.6 = (bf16[72,128]{1,0:T(8,128)(2,1)S(1)}, bf16[72,128]{1,0:T(8,128)(2,1)S(1)}, u32[]{:S(2)}, u32[]{:S(2)}) collective-permute-start(bf16[72,128]{1,0:T(8,128)(2,1)S(1)} %get-tuple-element.25), channel_id=1, source_target_pairs={{0,10},{2,8},{4,14},{6,12},{8,2},{10,0},{12,6},{14,4},{16,26},{18,... | collective-permute-start | bytes 55304 | tf_op jit(solution)/shard_map/ppermute | solution.py:268
  7.6 4.6 %collective-permute-start.1 = (bf16[72,128]{1,0:T(8,128)(2,1)S(1)}, bf16[72,128]{1,0:T(8,128)(2,1)S(1)}, u32[]{:S(2)}, u32[]{:S(2)}) collective-permute-start(bf16[72,128]{1,0:T(8,128)(2,1)S(1)} %get-tuple-element.22.refs_0_), channel_id=1, source_target_pairs={{0,2},{2,0},{4,6},{6,4},{1,3},{3,1},{5,7},{7,5},{8,10},{10,8},{12,... | collective-permute-start | bytes 55304 | tf_op jit(solution)/shard_map/ppermute | solution.py:16
  9.0 3.2 %collective-permute-start.3 = (bf16[72,128]{1,0:T(8,128)(2,1)S(1)}, bf16[72,128]{1,0:T(8,128)(2,1)S(1)}, u32[]{:S(2)}, u32[]{:S(2)}) collective-permute-start(bf16[72,128]{1,0:T(8,128)(2,1)S(1)} %collective-permute-done.2.refs_1_), channel_id=1, source_target_pairs={{0,2},{2,0},{4,6},{6,4},{1,3},{3,1},{5,7},{7,5},{8,10},{10,8},{12,... | collective-permute-start | bytes 55304 | tf_op jit(solution)/shard_map/ppermute | solution.py:16
  10.8 1.4 %collective-permute-start.5 = (bf16[72,128]{1,0:T(8,128)(2,1)S(1)}, bf16[72,128]{1,0:T(8,128)(2,1)S(1)}, u32[]{:S(2)}, u32[]{:S(2)}) collective-permute-start(bf16[72,128]{1,0:T(8,128)(2,1)S(1)} %collective-permute-done.4.refs_2_), channel_id=1, source_target_pairs={{0,2},{2,0},{4,6},{6,4},{1,3},{3,1},{5,7},{7,5},{8,10},{10,8},{12,... | collective-permute-start | bytes 55304 | tf_op jit(solution)/shard_map/ppermute | solution.py:16
  11.0 1.2 %collective-permute-start.7 = (bf16[72,128]{1,0:T(8,128)(2,1)S(1)}, bf16[72,128]{1,0:T(8,128)(2,1)S(1)}, u32[]{:S(2)}, u32[]{:S(2)}) collective-permute-start(bf16[72,128]{1,0:T(8,128)(2,1)S(1)} %collective-permute-done.6.refs_3_), channel_id=1, source_target_pairs={{0,2},{2,0},{4,6},{6,4},{1,3},{3,1},{5,7},{7,5},{8,10},{10,8},{12,... | collective-permute-start | bytes 55304 | tf_op jit(solution)/shard_map/ppermute | solution.py:16
  12.5 3.9 %collective-permute-start.8 = (bf16[96,128]{1,0:T(8,128)(2,1)S(1)}, bf16[96,128]{1,0:T(8,128)(2,1)S(1)}, u32[]{:S(2)}, u32[]{:S(2)}) collective-permute-start(bf16[96,128]{1,0:T(8,128)(2,1)S(1)} %get-tuple-element.28), channel_id=1, source_target_pairs={{0,1},{1,0},{2,3},{3,2},{4,5},{5,4},{6,7},{7,6},{8,9},{9,8},{10,11... | collective-permute-start | bytes 73736 | tf_op jit(solution)/shard_map/ppermute | solution.py:16
  14.1 3.4 %collective-permute-start.9 = (bf16[96,128]{1,0:T(8,128)(2,1)S(1)}, bf16[96,128]{1,0:T(8,128)(2,1)S(1)}, u32[]{:S(2)}, u32[]{:S(2)}) collective-permute-start(bf16[96,128]{1,0:T(8,128)(2,1)S(1)} %get-tuple-element.29), channel_id=1, source_target_pairs={{0,6},{2,4},{4,2},{6,0},{1,7},{3,5},{5,3},{7,1},{8,14},{10,12},{12... | collective-permute-start | bytes 73736 | tf_op jit(solution)/shard_map/ppermute | solution.py:16
  14.1 4.2 %collective-permute-start.10 = (bf16[96,128]{1,0:T(8,128)(2,1)S(1)}, bf16[96,128]{1,0:T(8,128)(2,1)S(1)}, u32[]{:S(2)}, u32[]{:S(2)}) collective-permute-start(bf16[96,128]{1,0:T(8,128)(2,1)S(1)} %get-tuple-element.30), channel_id=1, source_target_pairs={{0,7},{1,6},{2,5},{3,4},{4,3},{5,2},{6,1},{7,0},{8,15},{9,14},{10,... | collective-permute-start | bytes 73736 | tf_op jit(solution)/shard_map/ppermute | solution.py:305

commit v3 on v2

--- a/solution.py
+++ b/solution.py
@@ -10,6 +10,7 @@
 F32, BF16 = jnp.float32, jnp.bfloat16
 LANES = 128
 GRANT = 8 << 20
+PIECES = 3
 
 
 def flipped(value, axis, step):
@@ -52,13 +53,15 @@
     block_refs, (lat_ref, slots_ref, x_ref, sems) = rest[:-4], rest[-4:]
     width = LANES // planes
     band = lax.axis_index("band")
+    share = x_ref.shape[0] // PIECES
+    pieces = [pl.ds(i * share, share) for i in range(PIECES)]
     copies = [
         pltpu.make_async_copy(given, held, sems.at[i])
         for i, (given, held) in enumerate(
             (
                 (slots_hbm, slots_ref),
                 (lat_hbm, lat_ref),
-                (x_hbm, x_ref),
+                *((x_hbm.at[piece], x_ref.at[piece]) for piece in pieces),
                 (functions_hbm, functions_ref),
                 (vertical_hbm, vertical_ref),
             )
@@ -78,13 +81,15 @@
             slot_lanes_ref[...] = held
         hot = iota((waves, LANES), 0) == held[0:1]
         tables.append(jnp.where(hot, 1.0, 0.0).astype(BF16))
-    pair_rows = iota((2 * pairs, waves), 0) // 2
-    cutoff = jnp.zeros((2 * pairs, waves), jnp.int32)
+    pair_rows = iota((2 * pairs, waves), 0) >> 1
+    points = jnp.zeros((2 * pairs, waves), jnp.int32)
     copies[1].wait()
     for q in range(pairs):
-        cutoff = jnp.where(pair_rows == q, jnp.minimum(waves - 1, (lat_ref[0, q] - 1) // 2), cutoff)
+        points = jnp.where(pair_rows == q, lat_ref[0, q], points)
+    cutoff = jnp.minimum(waves - 1, (points - 1) >> 1)
     kept = iota((2 * pairs, waves), 1) <= cutoff
-    copies[2].wait()
+    for copy in copies[2 : 2 + PIECES]:
+        copy.wait()
     x = x_ref[...].astype(F32)
     rows = x.shape[0]
     following = pltpu.roll(x, rows - 1, 0)
@@ -105,8 +110,8 @@
         for plane in range(1, planes):
             block = jnp.where(plane_of == plane, mine[plane * count : (plane + 1) * count], block)
         block_ref[...] = block.astype(BF16)
-    copies[3].wait()
-    copies[4].wait()
+    for copy in copies[2 + PIECES :]:
+        copy.wait()
 
 
 def spread_kernel(dims, own_ref, other_ref, vertical_ref, out_ref, weights_ref, rows_ref):
@@ -181,7 +186,7 @@
         ref[...] = total_ref[:, at : at + 8, :].reshape(ref.shape).astype(BF16)
 
 
-def finish_kernel(dims, weights_ref, slot_lanes_ref, total_ref, x_ref, y_ref, xy_ref, out_ref, temps_ref, rows_ref):
+def finish_kernel(dims, weights_ref, slot_lanes_ref, total_ref, x_ref, y_ref, xy_ref, out_hbm, temps_ref, rows_ref, out_ref, sems):
     fields, levels, halves, slots, waves = dims
     planes = 2 * (levels // 4)
     width = LANES // planes
@@ -190,15 +195,24 @@
     count = 4 * fields
     from_x, from_y, from_xy = (r[...].astype(F32).reshape(count, 8, LANES) for r in (x_ref, y_ref, xy_ref))
     half = (lev * 2 + group) * halves + iota((8, LANES), 0)
-    valid = [slot_lanes_ref[...] + 2 * half + p <= waves - 1 for p in range(2)]
+    field_rows = levels * halves * 2
+    copies = []
 
     def store(p, f, level, c, value):
         start = ((p * (fields + 1) + f) * levels + level) * (2 * halves) + c
         rows_ref[pl.ds(start, halves, stride=2), :] = value[:halves]
 
-    for side in range(2):
+    def send(p, first, last):
+        start, stop = ((p * (fields + 1) + f) * field_rows for f in (first, last))
+        out_ref[start:stop] = rows_ref[start:stop, :slots].astype(BF16)
+        part = pl.ds(start, stop - start)
+        copies.append(pltpu.make_async_copy(out_ref.at[part], out_hbm.at[part], sems.at[len(copies)]))
+        copies[-1].start()
+
+    for p in range(2):
+        valid = slot_lanes_ref[...] + 2 * half + p <= waves - 1
         for f in range(fields):
-            for p in range(2):
+            for side in range(2):
                 n = (side * fields + f) * 2 + p
                 far_n = ((1 - side) * fields + f) * 2 + p
                 kept = jnp.concatenate(
@@ -206,7 +220,7 @@
                     axis=0,
                 )
                 for far, value in enumerate((kept + from_x[n], from_y[far_n] + from_xy[far_n])):
-                    value = jnp.where(valid[p], value, 0.0)
+                    value = jnp.where(valid, value, 0.0)
                     first = ((y ^ far) * 2 + (core ^ side)) * (levels // 4)
                     for plane in range(planes):
                         l, c = plane // 2, plane % 2
@@ -214,6 +228,7 @@
                         store(p, f, first + l, c, shifted)
                         if f == fields - 1:
                             temps_ref[first + l, 2 * p + c] = shifted
+        send(p, 0, fields)
     for p in range(2):
         for c in range(2):
             temps = [temps_ref[k, 2 * p + c] for k in range(levels)]
@@ -222,7 +237,9 @@
                 for k in range(level + 1, levels):
                     value += weights_ref[level * levels + k] * temps[k]
                 store(p, fields, level, c, value)
-    out_ref[...] = rows_ref[:, :slots].astype(BF16)
+        send(p, fields, fields + 1)
+    for copy in copies:
+        copy.wait()
 
 
 HBM = pl.BlockSpec(memory_space=pltpu.HBM)
@@ -256,7 +273,7 @@
             pltpu.SMEM(lat_points.shape, jnp.int32),
             pltpu.SMEM((1, wave_slots.size), jnp.int32),
             pltpu.VMEM(rows.shape, BF16),
-            pltpu.SemaphoreType.DMA((5,)),
+            pltpu.SemaphoreType.DMA((4 + PIECES,)),
         ],
         compiler_params=pltpu.CompilerParams(vmem_limit_bytes=GRANT),
         name="prepare",
@@ -282,25 +299,26 @@
     count = 4 * fields
     message = shape((count * 8, LANES), BF16)
     totals = shape((count, 24, LANES), F32)
-    direct = [(0, 0), *[(1, k) for k in steps]]
+    parts = [(own[k], (min(k, 1), k)) for k in range(bands)] + [(other[k], (1 - min(k, 1), k)) for k in range(bands)]
+    early, late = parts[: bands + 2], parts[bands + 2 :]
     before = pl.pallas_call(
-        functools.partial(sum_first_kernel, (fields, pairs, bands), direct),
-        in_specs=[VMEM] * (bands + 1),
+        functools.partial(sum_first_kernel, (fields, pairs, bands), [where for _, where in early]),
+        in_specs=[VMEM] * (len(early) + 1),
         out_specs=VMEM,
         out_shape=totals,
-        scratch_shapes=[pltpu.VMEM((bands, *block.shape), F32)],
+        scratch_shapes=[pltpu.VMEM((len(early), *block.shape), F32)],
         compiler_params=pltpu.CompilerParams(vmem_limit_bytes=GRANT),
         name="sum_first",
-    )(*[own[k] for k in range(bands)], table)
+    )(*[value for value, _ in early], table)
     total, to_x, to_y, to_xy = pl.pallas_call(
-        functools.partial(sum_kernel, (fields, pairs, bands), [(1 - side, k) for side, k in direct]),
-        in_specs=[VMEM] * (bands + 2),
+        functools.partial(sum_kernel, (fields, pairs, bands), [where for _, where in late]),
+        in_specs=[VMEM] * (len(late) + 2),
         out_specs=[VMEM] * 4,
         out_shape=[totals] + [message] * 3,
-        scratch_shapes=[pltpu.VMEM((bands, *block.shape), F32)],
+        scratch_shapes=[pltpu.VMEM((max(len(late), 1), *block.shape), F32)],
         compiler_params=pltpu.CompilerParams(vmem_limit_bytes=GRANT),
         name="sum",
-    )(*[other[k] for k in range(bands)], table, before)
+    )(*[value for value, _ in late], table, before)
 
     from_xy = lax.ppermute(to_xy, ("lev", "grp"), [(i, i ^ 7) for i in range(8)])
     from_x = flipped(to_x, "grp", 1)
@@ -310,9 +328,14 @@
     out = pl.pallas_call(
         functools.partial(finish_kernel, (fields, levels, own_halves, slots, waves)),
         in_specs=[VMEM] * 6,
-        out_specs=VMEM,
+        out_specs=HBM,
         out_shape=shape((out_rows, slots), BF16),
-        scratch_shapes=[pltpu.VMEM((levels, 4, 8, LANES), F32), pltpu.VMEM((out_rows, LANES), F32)],
+        scratch_shapes=[
+            pltpu.VMEM((levels, 4, 8, LANES), F32),
+            pltpu.VMEM((out_rows, LANES), F32),
+            pltpu.VMEM((out_rows, slots), BF16),
+            pltpu.SemaphoreType.DMA((4,)),
+        ],
         compiler_params=pltpu.CompilerParams(vmem_limit_bytes=GRANT),
         name="finish",
     )(weights, slot_lanes, total, from_x, from_y, from_xy)
@@ -322,7 +345,7 @@
 
 def fits(mesh, fourier, legendre):
     bands, levs, groups = (mesh.shape[a] for a in ("band", "lev", "grp"))
-    _, levels, _, _, _, pairs, waves = fourier.shape
+    fields, levels, _, _, _, pairs, waves = fourier.shape
     slots, _, halves, _, sums = legendre.shape
     planes = 2 * levels // levs
     return (
@@ -338,6 +361,7 @@
         and slots // bands % 8 == 0
         and 2 * pairs // bands % 8 == 0
         and sums % 8 == 0
+        and fields * planes * 2 * (pairs // bands) % (16 * PIECES) == 0
     )
 
 

time: 19.3 us -> 19.2 us (level)
  no operation moved by 1% of the time
where the time goes in v3:
time: 19.2 us; the launch traced here: 19.1 us
  starting transfers between devices  11.1 us (58%)
  waiting for transfers between devices  4.83 us (25%)
  Pallas kernels  3.1 us (16%)
    ppermute x7, starting transfers between devices, flipped(): lax.ppermute(value, axis, [(i, i ^ step) for i in range(lax.axis_size(axi...  5.37 us
    ppermute x3, starting transfers between devices, fast_body(): own[k] = lax.ppermute(blocks[k], ('band', 'lev'), crossed(k))  4 us
    ppermute x3, waiting for transfers between devices, fast_body(): own[k] = lax.ppermute(blocks[k], ('band', 'lev'), crossed(k))  2.35 us
    ppermute x7, waiting for transfers between devices, flipped(): lax.ppermute(value, axis, [(i, i ^ step) for i in range(lax.axis_size(axi...  1.7 us
    ppermute x1, starting transfers between devices, fast_body(): lax.ppermute(to_xy, ('lev', 'grp'), [(i, i ^ 7) for i in range(8)])  1.69 us
    pallas_call x1, Pallas kernels, fast_body(): pl.pallas_call(functools.partial(prepare_kernel, (fields, planes, pairs,...  1.07 us
    pallas_call x1, Pallas kernels, fast_body(): pl.pallas_call(functools.partial(finish_kernel, (fields, levels, own_halv...  0.88 us
    ppermute x1, waiting for transfers between devices, fast_body(): lax.ppermute(to_xy, ('lev', 'grp'), [(i, i ^ 7) for i in range(8)])  0.77 us
  transfers between devices with their start and end apart: 11, of which 6 were waited for; matrix products, arithmetic and copies ran while one was open for 0% of the time, Pallas kernels for 11%

profile of v3, /device:TPU:0, one launch (start us, length us, event | category | flops | bytes accessed | tf_op | source)
XLA Modules:
  0.0 19.1 jit_solution(2618099658996049352)
XLA Ops:
  0.0 2.4 %collective-permute-start = (bf16[576,48]{1,0:T(8,128)(2,1)}, bf16[576,48]{1,0:T(8,128)(2,1)S(1)}, u32[]{:S(2)}, u32[]{:S(2)}) collective-permute-start(bf16[576,48]{1,0:T(8,128)(2,1)} %bitcast.10), channel_id=1, source_target_pairs={{0,6},{2,4},{4,2},{6,0},{1,7},{3,5},{5,3},{7,1},{8,14},{10,12},{12... | collective-permute-start | bytes 165896 | tf_op jit(solution)/shard_map/ppermute | solution.py:17
  2.4 1.1 %prepare.1 = (s32[8,128]{1,0:T(8,128)S(1)}, bf16[576,48]{1,0:T(8,128)(2,1)S(1)}, f32[8,8]{1,0:T(8,128)S(1)}, bf16[72,128]{1,0:T(8,128)(2,1)S(1)}, bf16[72,128]{1...) custom-call(s32[1,12]{1,0:T(1,128)} %lat_hbm.1, s32[1,96]{1,0:T(1,128)} %bitcast.13, ...), custom_call_target="tpu_custom_call" | custom-call | tf_op jit(solution)/shard_map/prepare/pallas_call | solution.py:262
  3.5 2.9 %collective-permute-start.5 = (bf16[72,128]{1,0:T(8,128)(2,1)S(1)}, bf16[72,128]{1,0:T(8,128)(2,1)S(1)}, u32[]{:S(2)}, u32[]{:S(2)}) collective-permute-start(bf16[72,128]{1,0:T(8,128)(2,1)S(1)} %get-tuple-element.26), channel_id=1, source_target_pairs={{0,18},{2,16},{4,22},{6,20},{8,26},{10,24},{12,30},{14,28},{16,10}... | collective-permute-start | bytes 55304 | tf_op jit(solution)/shard_map/ppermute | solution.py:285
  6.4 1.1 %collective-permute-start.1 = (bf16[72,128]{1,0:T(8,128)(2,1)S(1)}, bf16[72,128]{1,0:T(8,128)(2,1)S(1)}, u32[]{:S(2)}, u32[]{:S(2)}) collective-permute-start(bf16[72,128]{1,0:T(8,128)(2,1)S(1)} %get-tuple-element.22), channel_id=1, source_target_pairs={{0,26},{2,24},{4,30},{6,28},{8,18},{10,16},{12,22},{14,20},{16,2},... | collective-permute-start | bytes 55304 | tf_op jit(solution)/shard_map/ppermute | solution.py:285
  7.5 0.0 collective-permute-start.3
  7.5 0.6 %collective-permute-start.6 = (bf16[72,128]{1,0:T(8,128)(2,1)S(1)}, bf16[72,128]{1,0:T(8,128)(2,1)S(1)}, u32[]{:S(2)}, u32[]{:S(2)}) collective-permute-start(bf16[72,128]{1,0:T(8,128)(2,1)S(1)} %get-tuple-element.25.refs_0_), channel_id=1, source_target_pairs={{0,2},{2,0},{4,6},{6,4},{1,3},{3,1},{5,7},{7,5},{8,10},{10,8},{12,... | collective-permute-start | bytes 55304 | tf_op jit(solution)/shard_map/ppermute | solution.py:17
  8.1 0.8 %collective-permute-done.5.refs_1_ = bf16[72,128]{1,0:T(8,128)(2,1)S(1)} collective-permute-done((bf16[72,128]{1,0:T(8,128)(2,1)S(1)}, bf16[72,128]{1,0:T(8,128)(2,1)S(1)}, u32[]{:S(2)}, u32[]{:S(2)}) %collective-permute-start.5) | collective-permute-done | bytes 18464 | tf_op jit(solution)/shard_map/ppermute | solution.py:285
  8.9 0.3 %collective-permute-start.7 = (bf16[72,128]{1,0:T(8,128)(2,1)S(1)}, bf16[72,128]{1,0:T(8,128)(2,1)S(1)}, u32[]{:S(2)}, u32[]{:S(2)}) collective-permute-start(bf16[72,128]{1,0:T(8,128)(2,1)S(1)} %collective-permute-done.5.refs_1_), channel_id=1, source_target_pairs={{0,2},{2,0},{4,6},{6,4},{1,3},{3,1},{5,7},{7,5},{8,10},{10,8},{12,... | collective-permute-start | bytes 55304 | tf_op jit(solution)/shard_map/ppermute | solution.py:17
  9.2 1.5 %collective-permute-done.1.refs_2_ = bf16[72,128]{1,0:T(8,128)(2,1)S(1)} collective-permute-done((bf16[72,128]{1,0:T(8,128)(2,1)S(1)}, bf16[72,128]{1,0:T(8,128)(2,1)S(1)}, u32[]{:S(2)}, u32[]{:S(2)}) %collective-permute-start.1) | collective-permute-done | bytes 18464 | tf_op jit(solution)/shard_map/ppermute | solution.py:285
  10.7 0.1 collective-permute-start.2
  10.8 0.1 collective-permute-done.3.refs_3_
  10.9 0.3 %collective-permute-start.4 = (bf16[72,128]{1,0:T(8,128)(2,1)S(1)}, bf16[72,128]{1,0:T(8,128)(2,1)S(1)}, u32[]{:S(2)}, u32[]{:S(2)}) collective-permute-start(bf16[72,128]{1,0:T(8,128)(2,1)S(1)} %collective-permute-done.3.refs_3_), channel_id=1, source_target_pairs={{0,2},{2,0},{4,6},{6,4},{1,3},{3,1},{5,7},{7,5},{8,10},{10,8},{12,... | collective-permute-start | bytes 55304 | tf_op jit(solution)/shard_map/ppermute | solution.py:17
  11.2 0.0 collective-permute-done.other_ref
  11.2 0.6 %spread.1 = (f32[2,1152,128]{2,1,0:T(8,128)S(1)}, f32[64,8,128]{2,1,0:T(8,128)S(1)}) custom-call(bf16[576,48]{1,0:T(8,128)(2,1)S(1)} %get-tuple-element.18.own_ref, bf16[576,48]{1,0:T(8,128)(2,1)S(1)} %collective-permute-done.other_ref, f32[8,8]{1,0:T(8,128)S(1)} %get-tuple-element.19.vertical_ref), custom_call_target="tpu_custom_call" | custom-call | tf_op jit(solution)/shard_map/spread/pallas_call | solution.py:286
  11.9 0.0 collective-permute-done.6.refs_4_
  11.9 0.0 collective-permute-done.7.refs_5_
  11.9 0.4 %sum_first.1.refs_3_ = f32[12,24,128]{2,1,0:T(8,128)S(1)} custom-call(bf16[72,128]{1,0:T(8,128)(2,1)S(1)} %get-tuple-element.25.refs_0_, bf16[72,128]{1,0:T(8,128)(2,1)S(1)} %collective-permute-done.5.refs_1_, bf16[72,128]{1,0:T(8,128)(2,1)S(1)} %collective-permute-done.1.refs_2_, bf16[72,128]{1,0:T(8,128)(2,1)S(1)} %collective-permute-done.3.refs_3_, ...), custom_call_target="tpu_custom_call" | custom-call | tf_op jit(solution)/shard_map/sum_first/pallas_call | solution.py:304
  12.3 0.0 collective-permute-done.2.refs_0_
  12.3 0.0 collective-permute-done.4.refs_1_
  12.3 0.1 sum.1
  12.4 1.5 %collective-permute-start.8 = (bf16[96,128]{1,0:T(8,128)(2,1)S(1)}, bf16[96,128]{1,0:T(8,128)(2,1)S(1)}, u32[]{:S(2)}, u32[]{:S(2)}) collective-permute-start(bf16[96,128]{1,0:T(8,128)(2,1)S(1)} %get-tuple-element.28), channel_id=1, source_target_pairs={{0,1},{1,0},{2,3},{3,2},{4,5},{5,4},{6,7},{7,6},{8,9},{9,8},{10,11... | collective-permute-start | bytes 73736 | tf_op jit(solution)/shard_map/ppermute | solution.py:17
  14.0 0.0 collective-permute-start.9
  14.0 1.7 %collective-permute-start.10 = (bf16[96,128]{1,0:T(8,128)(2,1)S(1)}, bf16[96,128]{1,0:T(8,128)(2,1)S(1)}, u32[]{:S(2)}, u32[]{:S(2)}) collective-permute-start(bf16[96,128]{1,0:T(8,128)(2,1)S(1)} %get-tuple-element.30), channel_id=1, source_target_pairs={{0,7},{1,6},{2,5},{3,4},{4,3},{5,2},{6,1},{7,0},{8,15},{9,14},{10,... | collective-permute-start | bytes 73736 | tf_op jit(solution)/shard_map/ppermute | solution.py:323
  15.7 0.6 %collective-permute-done.8.x_ref = bf16[96,128]{1,0:T(8,128)(2,1)S(1)} collective-permute-done((bf16[96,128]{1,0:T(8,128)(2,1)S(1)}, bf16[96,128]{1,0:T(8,128)(2,1)S(1)}, u32[]{:S(2)}, u32[]{:S(2)}) %collective-permute-start.8) | collective-permute-done | bytes 24608 | tf_op jit(solution)/shard_map/ppermute | solution.py:17
  16.3 1.1 %collective-permute-done.9.y_ref = bf16[96,128]{1,0:T(8,128)(2,1)S(1)} collective-permute-done((bf16[96,128]{1,0:T(8,128)(2,1)S(1)}, bf16[96,128]{1,0:T(8,128)(2,1)S(1)}, u32[]{:S(2)}, u32[]{:S(2)}) %collective-permute-start.9) | collective-permute-done | bytes 24608 | tf_op jit(solution)/shard_map/ppermute | solution.py:17
  17.4 0.8 %collective-permute-done.10.xy_ref = bf16[96,128]{1,0:T(8,128)(2,1)S(1)} collective-permute-done((bf16[96,128]{1,0:T(8,128)(2,1)S(1)}, bf16[96,128]{1,0:T(8,128)(2,1)S(1)}, u32[]{:S(2)}, u32[]{:S(2)}) %collective-permute-start.10) | collective-permute-done | bytes 24608 | tf_op jit(solution)/shard_map/ppermute | solution.py:323
  18.2 0.9 %finish.1 = bf16[768,24]{1,0:T(8,128)(2,1)} custom-call(f32[64,8,128]{2,1,0:T(8,128)S(1)} %get-tuple-element.20.weights_ref, s32[8,128]{1,0:T(8,128)S(1)} %get-tuple-element.21.slot_lanes_ref, f32[12,24,128]{2,1,0:T(8,128)S(1)} %get-tuple-element.27.total_ref, bf16[96,128]{1,0:T(8,128)(2,1)S(1)} %collective-permute-done.8.x_ref, ...), custom_call_target="tpu_custom_call" | custom-call | tf_op jit(solution)/shard_map/finish/pallas_call | solution.py:328
Async XLA Ops:
  0.0 11.2 %collective-permute-start = (bf16[576,48]{1,0:T(8,128)(2,1)}, bf16[576,48]{1,0:T(8,128)(2,1)S(1)}, u32[]{:S(2)}, u32[]{:S(2)}) collective-permute-start(bf16[576,48]{1,0:T(8,128)(2,1)} %bitcast.10), channel_id=1, source_target_pairs={{0,6},{2,4},{4,2},{6,0},{1,7},{3,5},{5,3},{7,1},{8,14},{10,12},{12... | collective-permute-start | bytes 165896 | tf_op jit(solution)/shard_map/ppermute | solution.py:17
  3.5 5.4 %collective-permute-start.5 = (bf16[72,128]{1,0:T(8,128)(2,1)S(1)}, bf16[72,128]{1,0:T(8,128)(2,1)S(1)}, u32[]{:S(2)}, u32[]{:S(2)}) collective-permute-start(bf16[72,128]{1,0:T(8,128)(2,1)S(1)} %get-tuple-element.26), channel_id=1, source_target_pairs={{0,18},{2,16},{4,22},{6,20},{8,26},{10,24},{12,30},{14,28},{16,10}... | collective-permute-start | bytes 55304 | tf_op jit(solution)/shard_map/ppermute | solution.py:285
  6.4 4.3 %collective-permute-start.1 = (bf16[72,128]{1,0:T(8,128)(2,1)S(1)}, bf16[72,128]{1,0:T(8,128)(2,1)S(1)}, u32[]{:S(2)}, u32[]{:S(2)}) collective-permute-start(bf16[72,128]{1,0:T(8,128)(2,1)S(1)} %get-tuple-element.22), channel_id=1, source_target_pairs={{0,26},{2,24},{4,30},{6,28},{8,18},{10,16},{12,22},{14,20},{16,2},... | collective-permute-start | bytes 55304 | tf_op jit(solution)/shard_map/ppermute | solution.py:285
  7.5 3.4 %collective-permute-start.3 = (bf16[72,128]{1,0:T(8,128)(2,1)S(1)}, bf16[72,128]{1,0:T(8,128)(2,1)S(1)}, u32[]{:S(2)}, u32[]{:S(2)}) collective-permute-start(bf16[72,128]{1,0:T(8,128)(2,1)S(1)} %get-tuple-element.23), channel_id=1, source_target_pairs={{0,10},{2,8},{4,14},{6,12},{8,2},{10,0},{12,6},{14,4},{16,26},{18,... | collective-permute-start | bytes 55304 | tf_op jit(solution)/shard_map/ppermute | solution.py:285
  7.5 4.3 %collective-permute-start.6 = (bf16[72,128]{1,0:T(8,128)(2,1)S(1)}, bf16[72,128]{1,0:T(8,128)(2,1)S(1)}, u32[]{:S(2)}, u32[]{:S(2)}) collective-permute-start(bf16[72,128]{1,0:T(8,128)(2,1)S(1)} %get-tuple-element.25.refs_0_), channel_id=1, source_target_pairs={{0,2},{2,0},{4,6},{6,4},{1,3},{3,1},{5,7},{7,5},{8,10},{10,8},{12,... | collective-permute-start | bytes 55304 | tf_op jit(solution)/shard_map/ppermute | solution.py:17
  8.9 3.0 %collective-permute-start.7 = (bf16[72,128]{1,0:T(8,128)(2,1)S(1)}, bf16[72,128]{1,0:T(8,128)(2,1)S(1)}, u32[]{:S(2)}, u32[]{:S(2)}) collective-permute-start(bf16[72,128]{1,0:T(8,128)(2,1)S(1)} %collective-permute-done.5.refs_1_), channel_id=1, source_target_pairs={{0,2},{2,0},{4,6},{6,4},{1,3},{3,1},{5,7},{7,5},{8,10},{10,8},{12,... | collective-permute-start | bytes 55304 | tf_op jit(solution)/shard_map/ppermute | solution.py:17
  10.7 1.6 %collective-permute-start.2 = (bf16[72,128]{1,0:T(8,128)(2,1)S(1)}, bf16[72,128]{1,0:T(8,128)(2,1)S(1)}, u32[]{:S(2)}, u32[]{:S(2)}) collective-permute-start(bf16[72,128]{1,0:T(8,128)(2,1)S(1)} %collective-permute-done.1.refs_2_), channel_id=1, source_target_pairs={{0,2},{2,0},{4,6},{6,4},{1,3},{3,1},{5,7},{7,5},{8,10},{10,8},{12,... | collective-permute-start | bytes 55304 | tf_op jit(solution)/shard_map/ppermute | solution.py:17
  10.9 1.4 %collective-permute-start.4 = (bf16[72,128]{1,0:T(8,128)(2,1)S(1)}, bf16[72,128]{1,0:T(8,128)(2,1)S(1)}, u32[]{:S(2)}, u32[]{:S(2)}) collective-permute-start(bf16[72,128]{1,0:T(8,128)(2,1)S(1)} %collective-permute-done.3.refs_3_), channel_id=1, source_target_pairs={{0,2},{2,0},{4,6},{6,4},{1,3},{3,1},{5,7},{7,5},{8,10},{10,8},{12,... | collective-permute-start | bytes 55304 | tf_op jit(solution)/shard_map/ppermute | solution.py:17
  12.4 3.9 %collective-permute-start.8 = (bf16[96,128]{1,0:T(8,128)(2,1)S(1)}, bf16[96,128]{1,0:T(8,128)(2,1)S(1)}, u32[]{:S(2)}, u32[]{:S(2)}) collective-permute-start(bf16[96,128]{1,0:T(8,128)(2,1)S(1)} %get-tuple-element.28), channel_id=1, source_target_pairs={{0,1},{1,0},{2,3},{3,2},{4,5},{5,4},{6,7},{7,6},{8,9},{9,8},{10,11... | collective-permute-start | bytes 73736 | tf_op jit(solution)/shard_map/ppermute | solution.py:17
  14.0 3.4 %collective-permute-start.9 = (bf16[96,128]{1,0:T(8,128)(2,1)S(1)}, bf16[96,128]{1,0:T(8,128)(2,1)S(1)}, u32[]{:S(2)}, u32[]{:S(2)}) collective-permute-start(bf16[96,128]{1,0:T(8,128)(2,1)S(1)} %get-tuple-element.29), channel_id=1, source_target_pairs={{0,6},{2,4},{4,2},{6,0},{1,7},{3,5},{5,3},{7,1},{8,14},{10,12},{12... | collective-permute-start | bytes 73736 | tf_op jit(solution)/shard_map/ppermute | solution.py:17
  14.0 4.2 %collective-permute-start.10 = (bf16[96,128]{1,0:T(8,128)(2,1)S(1)}, bf16[96,128]{1,0:T(8,128)(2,1)S(1)}, u32[]{:S(2)}, u32[]{:S(2)}) collective-permute-start(bf16[96,128]{1,0:T(8,128)(2,1)S(1)} %get-tuple-element.30), channel_id=1, source_target_pairs={{0,7},{1,6},{2,5},{3,4},{4,3},{5,2},{6,1},{7,0},{8,15},{9,14},{10,... | collective-permute-start | bytes 73736 | tf_op jit(solution)/shard_map/ppermute | solution.py:323

commit v4 on v3

--- a/solution.py
+++ b/solution.py
@@ -42,6 +42,10 @@
     bands, levs = lax.axis_size("band"), lax.axis_size("lev")
     to = rounds(bands)[k - 1]
     return [(b * levs + v, to[b] * levs + (v ^ 1)) for b in range(bands) for v in range(levs)]
+
+
+def round_the_square(levs, late):
+    return [(v * 2 + g, ((v ^ 1) if g == late else (v ^ 3)) * 2 + 1 - g) for v in range(levs) for g in range(2)]
 
 
 def iota(shape, dim):
@@ -114,7 +118,7 @@
         copy.wait()
 
 
-def spread_kernel(dims, own_ref, other_ref, vertical_ref, out_ref, weights_ref, rows_ref):
+def spread_kernel(dims, own_ref, core_ref, other_ref, vertical_ref, out_ref, weights_ref, rows_ref):
     planes, slots, halves, sums = dims
     width = LANES // planes
     group = lax.axis_index("grp")
@@ -124,14 +128,19 @@
     for level in range(levels):
         for k in range(level, levels):
             weights_ref[level * levels + k] = jnp.broadcast_to(vertical_ref[level : level + 1, k : k + 1], (8, LANES))
-    for side, ref in enumerate((own_ref, other_ref)):
+    for side, ref in enumerate((own_ref, other_ref, core_ref)):
         rows_ref[side, :, :sums] = ref[...].astype(F32)
+    for side in range(2):
         for p in range(2):
             for first in range(0, halves, planes):
                 pieces = []
                 for part in range(planes):
                     start = (first + part) * 2 + p
-                    pieces.append(rows_ref[side, pl.ds(start, slots, stride=2 * halves), :])
+                    piece = rows_ref[side, pl.ds(start, slots, stride=2 * halves), :]
+                    if side == 0:
+                        across = rows_ref[2, pl.ds(start, slots, stride=2 * halves), :]
+                        piece = jnp.where(group == (first + part) // own, piece, across)
+                    pieces.append(piece)
                     if width > slots:
                         pieces.append(jnp.zeros((width - slots, LANES), F32))
                 turned = jnp.concatenate(pieces, axis=0).T[:sums]
@@ -174,7 +183,7 @@
 
 
 def sum_kernel(dims, parts, *refs):
-    block_refs, (table_ref, before_ref, total_ref, x_ref, y_ref, xy_ref, rows_ref) = refs[:-7], refs[-7:]
+    block_refs, (table_ref, before_ref, total_ref, soon_ref, y_ref, late_ref, rows_ref) = refs[:-7], refs[-7:]
     for i, block_ref in enumerate(block_refs):
         rows_ref[i] = block_ref[...].astype(F32)
     for p in range(2):
@@ -182,18 +191,20 @@
         add_products(dims, parts, table_ref, rows_ref, p, totals)
         for i, total in enumerate(totals):
             total_ref[2 * i + p] = total
-    for at, ref in ((0, x_ref), (8, y_ref), (16, xy_ref)):
-        ref[...] = total_ref[:, at : at + 8, :].reshape(ref.shape).astype(BF16)
-
-
-def finish_kernel(dims, weights_ref, slot_lanes_ref, total_ref, x_ref, y_ref, xy_ref, out_hbm, temps_ref, rows_ref, out_ref, sems):
+    group = lax.axis_index("grp")
+    for at, ref in ((16 * group, soon_ref), (8, y_ref), (16 - 16 * group, late_ref)):
+        ref[...] = total_ref[:, pl.ds(pl.multiple_of(at, 8), 8), :].reshape(ref.shape).astype(BF16)
+
+
+def finish_kernel(dims, weights_ref, slot_lanes_ref, total_ref, soon_ref, y_ref, late_ref, out_hbm, temps_ref, rows_ref, out_ref, sems):
     fields, levels, halves, slots, waves = dims
     planes = 2 * (levels // 4)
     width = LANES // planes
     lev, group = lax.axis_index("lev"), lax.axis_index("grp")
     y, core = lev // 2, lev % 2
     count = 4 * fields
-    from_x, from_y, from_xy = (r[...].astype(F32).reshape(count, 8, LANES) for r in (x_ref, y_ref, xy_ref))
+    soon, from_y, late = (r[...].astype(F32).reshape(count, 8, LANES) for r in (soon_ref, y_ref, late_ref))
+    from_x, from_xy = jnp.where(group == 0, late, soon), jnp.where(group == 0, soon, late)
     half = (lev * 2 + group) * halves + iota((8, LANES), 0)
     field_rows = levels * halves * 2
     copies = []
@@ -219,7 +230,7 @@
                     [total_ref[n, 6:8, :], total_ref[n, 14:16, :], total_ref[n, 22:24, :], jnp.zeros((2, LANES), F32)],
                     axis=0,
                 )
-                for far, value in enumerate((kept + from_x[n], from_y[far_n] + from_xy[far_n])):
+                for far, value in enumerate((kept + from_x[far_n], from_y[far_n] + from_xy[far_n])):
                     value = jnp.where(valid, value, 0.0)
                     first = ((y ^ far) * 2 + (core ^ side)) * (levels // 4)
                     for plane in range(planes):
@@ -283,15 +294,16 @@
     own = {0: blocks[0]}
     for k in steps:
         own[k] = lax.ppermute(blocks[k], ("band", "lev"), crossed(k))
+    core_functions = flipped(functions, "lev", 1)
     table, weights = pl.pallas_call(
         functools.partial(spread_kernel, (planes, slots, halves, sums)),
-        in_specs=[VMEM] * 3,
+        in_specs=[VMEM] * 4,
         out_specs=[VMEM] * 2,
         out_shape=[shape((2, sums * 24, LANES), F32), shape((levels * levels, 8, LANES), F32)],
-        scratch_shapes=[pltpu.VMEM((2, slots * halves * 2, LANES), F32)],
+        scratch_shapes=[pltpu.VMEM((3, slots * halves * 2, LANES), F32)],
         compiler_params=pltpu.CompilerParams(vmem_limit_bytes=GRANT),
         name="spread",
-    )(functions, other_functions, vertical)
+    )(functions, core_functions, other_functions, vertical)
     other = {}
     for k in (0, *steps):
         other[k] = flipped(own[k], "lev", 1)
@@ -300,7 +312,7 @@
     message = shape((count * 8, LANES), BF16)
     totals = shape((count, 24, LANES), F32)
     parts = [(own[k], (min(k, 1), k)) for k in range(bands)] + [(other[k], (1 - min(k, 1), k)) for k in range(bands)]
-    early, late = parts[: bands + 2], parts[bands + 2 :]
+    early, others = parts[: bands + 2], parts[bands + 2 :]
     before = pl.pallas_call(
         functools.partial(sum_first_kernel, (fields, pairs, bands), [where for _, where in early]),
         in_specs=[VMEM] * (len(early) + 1),
@@ -310,19 +322,20 @@
         compiler_params=pltpu.CompilerParams(vmem_limit_bytes=GRANT),
         name="sum_first",
     )(*[value for value, _ in early], table)
-    total, to_x, to_y, to_xy = pl.pallas_call(
-        functools.partial(sum_kernel, (fields, pairs, bands), [where for _, where in late]),
-        in_specs=[VMEM] * (len(late) + 2),
+    total, soon, to_y, late = pl.pallas_call(
+        functools.partial(sum_kernel, (fields, pairs, bands), [where for _, where in others]),
+        in_specs=[VMEM] * (len(others) + 2),
         out_specs=[VMEM] * 4,
         out_shape=[totals] + [message] * 3,
-        scratch_shapes=[pltpu.VMEM((max(len(late), 1), *block.shape), F32)],
+        scratch_shapes=[pltpu.VMEM((max(len(others), 1), *block.shape), F32)],
         compiler_params=pltpu.CompilerParams(vmem_limit_bytes=GRANT),
         name="sum",
-    )(*[value for value, _ in late], table, before)
-
-    from_xy = lax.ppermute(to_xy, ("lev", "grp"), [(i, i ^ 7) for i in range(8)])
-    from_x = flipped(to_x, "grp", 1)
+    )(*[value for value, _ in others], table, before)
+
+    levs = lax.axis_size("lev")
+    from_soon = lax.ppermute(soon, ("lev", "grp"), round_the_square(levs, 0))
     from_y = flipped(to_y, "lev", 3)
+    from_late = lax.ppermute(late, ("lev", "grp"), round_the_square(levs, 1))
     own_halves = halves // 2
     out_rows = 2 * (fields + 1) * levels * own_halves * 2
     out = pl.pallas_call(
@@ -332,13 +345,13 @@
         out_shape=shape((out_rows, slots), BF16),
         scratch_shapes=[
             pltpu.VMEM((levels, 4, 8, LANES), F32),
-            pltpu.VMEM((out_rows, LANES), F32),
+            pltpu.VMEM((out_rows + 16, LANES), F32),
             pltpu.VMEM((out_rows, slots), BF16),
             pltpu.SemaphoreType.DMA((4,)),
         ],
         compiler_params=pltpu.CompilerParams(vmem_limit_bytes=GRANT),
         name="finish",
-    )(weights, slot_lanes, total, from_x, from_y, from_xy)
+    )(weights, slot_lanes, total, from_soon, from_y, from_late)
     out = out.reshape(2, fields + 1, levels, own_halves, 2, slots)
     return out.transpose(5, 0, 1, 2, 4, 3)
 

time: 19.2 us -> 20.7 us (1.078)
  waiting for transfers between devices: 4.83 us -> 6.47 us
    ppermute x1 -> x2, waiting for transfers between devices: 0.77 us -> 3.57 us  [the longest x1 2.63 us: fast_body(): from_soon = lax.ppermute(soon, ('lev', 'grp'), round_the_square(levs, 0))]
    ppermute x7, waiting for transfers between devices: 1.7 us -> 0.59 us  [flipped(): lax.ppermute(value, axis, [(i, i ^ step) for i in range(lax.axis_size(axi...]
    ppermute x7, starting transfers between devices: 5.37 us -> 4.66 us  [flipped(): lax.ppermute(value, axis, [(i, i ^ step) for i in range(lax.axis_size(axi...]
    ppermute x1 -> x2, starting transfers between devices: 1.69 us -> 2.38 us  [the longest x1 2.38 us: fast_body(): from_late = lax.ppermute(late, ('lev', 'grp'), round_the_square(levs, 1))]
  transfers between devices with their start and end apart: 11 -> 12, of which waited for: 6 -> 5; matrix products, arithmetic and copies ran while one was open for 0% -> 0% of each run, Pallas kernels for 11% -> 5%
where the time goes in v4:
time: 20.7 us; the launch traced here: 20.6 us
  starting transfers between devices  10.9 us (53%)
  waiting for transfers between devices  6.47 us (31%)
  Pallas kernels  3.13 us (15%)
    ppermute x7, starting transfers between devices, flipped(): lax.ppermute(value, axis, [(i, i ^ step) for i in range(lax.axis_size(axi...  4.66 us
    ppermute x3, starting transfers between devices, fast_body(): own[k] = lax.ppermute(blocks[k], ('band', 'lev'), crossed(k))  3.88 us
    ppermute x1, waiting for transfers between devices, fast_body(): from_soon = lax.ppermute(soon, ('lev', 'grp'), round_the_square(levs, 0))  2.63 us
    ppermute x1, starting transfers between devices, fast_body(): from_late = lax.ppermute(late, ('lev', 'grp'), round_the_square(levs, 1))  2.38 us
    ppermute x3, waiting for transfers between devices, fast_body(): own[k] = lax.ppermute(blocks[k], ('band', 'lev'), crossed(k))  2.31 us
    pallas_call x1, Pallas kernels, fast_body(): pl.pallas_call(functools.partial(prepare_kernel, (fields, planes, pairs,...  1.06 us
    ppermute x1, waiting for transfers between devices, fast_body(): from_late = lax.ppermute(late, ('lev', 'grp'), round_the_square(levs, 1))  0.94 us
    pallas_call x1, Pallas kernels, fast_body(): pl.pallas_call(functools.partial(finish_kernel, (fields, levels, own_halv...  0.88 us
  transfers between devices with their start and end apart: 12, of which 5 were waited for; matrix products, arithmetic and copies ran while one was open for 0% of the time, Pallas kernels for 5%

profile of v4, /device:TPU:0, one launch (start us, length us, event | category | flops | bytes accessed | tf_op | source)
XLA Modules:
  0.0 20.6 jit_solution(10814544343347456689)
XLA Ops:
  0.0 1.1 %prepare.1 = (s32[8,128]{1,0:T(8,128)S(1)}, bf16[576,48]{1,0:T(8,128)(2,1)S(1)}, f32[8,8]{1,0:T(8,128)S(1)}, bf16[72,128]{1,0:T(8,128)(2,1)S(1)}, bf16[72,128]{1...) custom-call(s32[1,12]{1,0:T(1,128)} %lat_hbm.1, s32[1,96]{1,0:T(1,128)} %bitcast.13, ...), custom_call_target="tpu_custom_call" | custom-call | tf_op jit(solution)/shard_map/prepare/pallas_call | solution.py:273
  1.1 0.6 %collective-permute-start = (bf16[576,48]{1,0:T(8,128)(2,1)S(1)}, bf16[576,48]{1,0:T(8,128)(2,1)S(1)}, u32[]{:S(2)}, u32[]{:S(2)}) collective-permute-start(bf16[576,48]{1,0:T(8,128)(2,1)S(1)} %get-tuple-element.18.own_ref), channel_id=1, source_target_pairs={{0,2},{2,0},{4,6},{6,4},{1,3},{3,1},{5,7},{7,5},{8,10},{10,8},{12,... | collective-permute-start | bytes 165896 | tf_op jit(solution)/shard_map/ppermute | solution.py:17
  1.6 2.6 %collective-permute-start.1 = (bf16[576,48]{1,0:T(8,128)(2,1)}, bf16[576,48]{1,0:T(8,128)(2,1)S(1)}, u32[]{:S(2)}, u32[]{:S(2)}) collective-permute-start(bf16[576,48]{1,0:T(8,128)(2,1)} %bitcast.11), channel_id=1, source_target_pairs={{0,6},{2,4},{4,2},{6,0},{1,7},{3,5},{5,3},{7,1},{8,14},{10,12},{12... | collective-permute-start | bytes 165896 | tf_op jit(solution)/shard_map/ppermute | solution.py:17
  4.3 2.3 %collective-permute-start.6 = (bf16[72,128]{1,0:T(8,128)(2,1)S(1)}, bf16[72,128]{1,0:T(8,128)(2,1)S(1)}, u32[]{:S(2)}, u32[]{:S(2)}) collective-permute-start(bf16[72,128]{1,0:T(8,128)(2,1)S(1)} %get-tuple-element.26), channel_id=1, source_target_pairs={{0,18},{2,16},{4,22},{6,20},{8,26},{10,24},{12,30},{14,28},{16,10}... | collective-permute-start | bytes 55304 | tf_op jit(solution)/shard_map/ppermute | solution.py:296
  6.5 1.3 %collective-permute-start.2 = (bf16[72,128]{1,0:T(8,128)(2,1)S(1)}, bf16[72,128]{1,0:T(8,128)(2,1)S(1)}, u32[]{:S(2)}, u32[]{:S(2)}) collective-permute-start(bf16[72,128]{1,0:T(8,128)(2,1)S(1)} %get-tuple-element.22), channel_id=1, source_target_pairs={{0,26},{2,24},{4,30},{6,28},{8,18},{10,16},{12,22},{14,20},{16,2},... | collective-permute-start | bytes 55304 | tf_op jit(solution)/shard_map/ppermute | solution.py:296
  7.8 0.3 %collective-permute-start.4 = (bf16[72,128]{1,0:T(8,128)(2,1)S(1)}, bf16[72,128]{1,0:T(8,128)(2,1)S(1)}, u32[]{:S(2)}, u32[]{:S(2)}) collective-permute-start(bf16[72,128]{1,0:T(8,128)(2,1)S(1)} %get-tuple-element.23), channel_id=1, source_target_pairs={{0,10},{2,8},{4,14},{6,12},{8,2},{10,0},{12,6},{14,4},{16,26},{18,... | collective-permute-start | bytes 55304 | tf_op jit(solution)/shard_map/ppermute | solution.py:296
  8.1 1.1 %collective-permute-done.6.refs_1_ = bf16[72,128]{1,0:T(8,128)(2,1)S(1)} collective-permute-done((bf16[72,128]{1,0:T(8,128)(2,1)S(1)}, bf16[72,128]{1,0:T(8,128)(2,1)S(1)}, u32[]{:S(2)}, u32[]{:S(2)}) %collective-permute-start.6) | collective-permute-done | bytes 18464 | tf_op jit(solution)/shard_map/ppermute | solution.py:296
  9.2 0.2 collective-permute-start.7
  9.4 1.2 %collective-permute-done.2.refs_2_ = bf16[72,128]{1,0:T(8,128)(2,1)S(1)} collective-permute-done((bf16[72,128]{1,0:T(8,128)(2,1)S(1)}, bf16[72,128]{1,0:T(8,128)(2,1)S(1)}, u32[]{:S(2)}, u32[]{:S(2)}) %collective-permute-start.2) | collective-permute-done | bytes 18464 | tf_op jit(solution)/shard_map/ppermute | solution.py:296
  10.6 0.4 %collective-permute-start.8 = (bf16[72,128]{1,0:T(8,128)(2,1)S(1)}, bf16[72,128]{1,0:T(8,128)(2,1)S(1)}, u32[]{:S(2)}, u32[]{:S(2)}) collective-permute-start(bf16[72,128]{1,0:T(8,128)(2,1)S(1)} %collective-permute-done.6.refs_1_), channel_id=1, source_target_pairs={{0,2},{2,0},{4,6},{6,4},{1,3},{3,1},{5,7},{7,5},{8,10},{10,8},{12,... | collective-permute-start | bytes 55304 | tf_op jit(solution)/shard_map/ppermute | solution.py:17
  11.0 0.0 collective-permute-done.4.refs_3_
  11.1 0.2 collective-permute-start.3
  11.2 0.0 collective-permute-done.core_ref
  11.2 0.3 %collective-permute-start.5 = (bf16[72,128]{1,0:T(8,128)(2,1)S(1)}, bf16[72,128]{1,0:T(8,128)(2,1)S(1)}, u32[]{:S(2)}, u32[]{:S(2)}) collective-permute-start(bf16[72,128]{1,0:T(8,128)(2,1)S(1)} %collective-permute-done.4.refs_3_), channel_id=1, source_target_pairs={{0,2},{2,0},{4,6},{6,4},{1,3},{3,1},{5,7},{7,5},{8,10},{10,8},{12,... | collective-permute-start | bytes 55304 | tf_op jit(solution)/shard_map/ppermute | solution.py:17
  11.6 0.0 collective-permute-done.1.other_ref
  11.6 0.6 %spread.1 = (f32[2,1152,128]{2,1,0:T(8,128)S(1)}, f32[64,8,128]{2,1,0:T(8,128)S(1)}) custom-call(bf16[576,48]{1,0:T(8,128)(2,1)S(1)} %get-tuple-element.18.own_ref, bf16[576,48]{1,0:T(8,128)(2,1)S(1)} %collective-permute-done.core_ref, bf16[576,48]{1,0:T(8,128)(2,1)S(1)} %collective-permute-done.1.other_ref, f32[8,8]{1,0:T(8,128)S(1)} %get-tuple-element.19.vertical_ref), custom_call_target="tpu_custom_call" | custom-call | tf_op jit(solution)/shard_map/spread/pallas_call | solution.py:298
  12.2 0.0 collective-permute-done.7.refs_4_
  12.2 0.0 collective-permute-done.8.refs_5_
  12.2 0.4 %sum_first.1.refs_3_ = f32[12,24,128]{2,1,0:T(8,128)S(1)} custom-call(bf16[72,128]{1,0:T(8,128)(2,1)S(1)} %get-tuple-element.25.refs_0_, bf16[72,128]{1,0:T(8,128)(2,1)S(1)} %collective-permute-done.6.refs_1_, bf16[72,128]{1,0:T(8,128)(2,1)S(1)} %collective-permute-done.2.refs_2_, bf16[72,128]{1,0:T(8,128)(2,1)S(1)} %collective-permute-done.4.refs_3_, ...), custom_call_target="tpu_custom_call" | custom-call | tf_op jit(solution)/shard_map/sum_first/pallas_call | solution.py:316
  12.6 0.0 collective-permute-done.3.refs_0_
  12.6 0.0 collective-permute-done.5.refs_1_
  12.7 0.2 sum.1
  12.8 0.4 %collective-permute-start.10 = (bf16[96,128]{1,0:T(8,128)(2,1)S(1)}, bf16[96,128]{1,0:T(8,128)(2,1)S(1)}, u32[]{:S(2)}, u32[]{:S(2)}) collective-permute-start(bf16[96,128]{1,0:T(8,128)(2,1)S(1)} %get-tuple-element.29), channel_id=1, source_target_pairs={{0,6},{2,4},{4,2},{6,0},{1,7},{3,5},{5,3},{7,1},{8,14},{10,12},{12... | collective-permute-start | bytes 73736 | tf_op jit(solution)/shard_map/ppermute | solution.py:17
  13.2 2.4 %collective-permute-start.11 = (bf16[96,128]{1,0:T(8,128)(2,1)S(1)}, bf16[96,128]{1,0:T(8,128)(2,1)S(1)}, u32[]{:S(2)}, u32[]{:S(2)}) collective-permute-start(bf16[96,128]{1,0:T(8,128)(2,1)S(1)} %get-tuple-element.30), channel_id=1, source_target_pairs={{0,7},{1,2},{2,5},{3,0},{4,3},{5,6},{6,1},{7,4},{8,15},{9,10},{10,... | collective-permute-start | bytes 73736 | tf_op jit(solution)/shard_map/ppermute | solution.py:338
  15.6 0.0 collective-permute-start.9
  15.6 0.6 %collective-permute-done.10.y_ref = bf16[96,128]{1,0:T(8,128)(2,1)S(1)} collective-permute-done((bf16[96,128]{1,0:T(8,128)(2,1)S(1)}, bf16[96,128]{1,0:T(8,128)(2,1)S(1)}, u32[]{:S(2)}, u32[]{:S(2)}) %collective-permute-start.10) | collective-permute-done | bytes 24608 | tf_op jit(solution)/shard_map/ppermute | solution.py:17
  16.1 0.9 %collective-permute-done.11.late_ref = bf16[96,128]{1,0:T(8,128)(2,1)S(1)} collective-permute-done((bf16[96,128]{1,0:T(8,128)(2,1)S(1)}, bf16[96,128]{1,0:T(8,128)(2,1)S(1)}, u32[]{:S(2)}, u32[]{:S(2)}) %collective-permute-start.11) | collective-permute-done | bytes 24608 | tf_op jit(solution)/shard_map/ppermute | solution.py:338
  17.1 2.6 %collective-permute-done.9.soon_ref = bf16[96,128]{1,0:T(8,128)(2,1)S(1)} collective-permute-done((bf16[96,128]{1,0:T(8,128)(2,1)S(1)}, bf16[96,128]{1,0:T(8,128)(2,1)S(1)}, u32[]{:S(2)}, u32[]{:S(2)}) %collective-permute-start.9) | collective-permute-done | bytes 24608 | tf_op jit(solution)/shard_map/ppermute | solution.py:336
  19.7 0.9 %finish.1 = bf16[768,24]{1,0:T(8,128)(2,1)} custom-call(f32[64,8,128]{2,1,0:T(8,128)S(1)} %get-tuple-element.20.weights_ref, s32[8,128]{1,0:T(8,128)S(1)} %get-tuple-element.21.slot_lanes_ref, f32[12,24,128]{2,1,0:T(8,128)S(1)} %get-tuple-element.27.total_ref, bf16[96,128]{1,0:T(8,128)(2,1)S(1)} %collective-permute-done.9.soon_ref, ...), custom_call_target="tpu_custom_call" | custom-call | tf_op jit(solution)/shard_map/finish/pallas_call | solution.py:341
Async XLA Ops:
  1.1 10.2 %collective-permute-start = (bf16[576,48]{1,0:T(8,128)(2,1)S(1)}, bf16[576,48]{1,0:T(8,128)(2,1)S(1)}, u32[]{:S(2)}, u32[]{:S(2)}) collective-permute-start(bf16[576,48]{1,0:T(8,128)(2,1)S(1)} %get-tuple-element.18.own_ref), channel_id=1, source_target_pairs={{0,2},{2,0},{4,6},{6,4},{1,3},{3,1},{5,7},{7,5},{8,10},{10,8},{12,... | collective-permute-start | bytes 165896 | tf_op jit(solution)/shard_map/ppermute | solution.py:17
  1.6 9.9 %collective-permute-start.1 = (bf16[576,48]{1,0:T(8,128)(2,1)}, bf16[576,48]{1,0:T(8,128)(2,1)S(1)}, u32[]{:S(2)}, u32[]{:S(2)}) collective-permute-start(bf16[576,48]{1,0:T(8,128)(2,1)} %bitcast.11), channel_id=1, source_target_pairs={{0,6},{2,4},{4,2},{6,0},{1,7},{3,5},{5,3},{7,1},{8,14},{10,12},{12... | collective-permute-start | bytes 165896 | tf_op jit(solution)/shard_map/ppermute | solution.py:17
  4.3 5.0 %collective-permute-start.6 = (bf16[72,128]{1,0:T(8,128)(2,1)S(1)}, bf16[72,128]{1,0:T(8,128)(2,1)S(1)}, u32[]{:S(2)}, u32[]{:S(2)}) collective-permute-start(bf16[72,128]{1,0:T(8,128)(2,1)S(1)} %get-tuple-element.26), channel_id=1, source_target_pairs={{0,18},{2,16},{4,22},{6,20},{8,26},{10,24},{12,30},{14,28},{16,10}... | collective-permute-start | bytes 55304 | tf_op jit(solution)/shard_map/ppermute | solution.py:296
  6.5 4.1 %collective-permute-start.2 = (bf16[72,128]{1,0:T(8,128)(2,1)S(1)}, bf16[72,128]{1,0:T(8,128)(2,1)S(1)}, u32[]{:S(2)}, u32[]{:S(2)}) collective-permute-start(bf16[72,128]{1,0:T(8,128)(2,1)S(1)} %get-tuple-element.22), channel_id=1, source_target_pairs={{0,26},{2,24},{4,30},{6,28},{8,18},{10,16},{12,22},{14,20},{16,2},... | collective-permute-start | bytes 55304 | tf_op jit(solution)/shard_map/ppermute | solution.py:296
  7.8 3.3 %collective-permute-start.4 = (bf16[72,128]{1,0:T(8,128)(2,1)S(1)}, bf16[72,128]{1,0:T(8,128)(2,1)S(1)}, u32[]{:S(2)}, u32[]{:S(2)}) collective-permute-start(bf16[72,128]{1,0:T(8,128)(2,1)S(1)} %get-tuple-element.23), channel_id=1, source_target_pairs={{0,10},{2,8},{4,14},{6,12},{8,2},{10,0},{12,6},{14,4},{16,26},{18,... | collective-permute-start | bytes 55304 | tf_op jit(solution)/shard_map/ppermute | solution.py:296
  9.2 3.0 %collective-permute-start.7 = (bf16[72,128]{1,0:T(8,128)(2,1)S(1)}, bf16[72,128]{1,0:T(8,128)(2,1)S(1)}, u32[]{:S(2)}, u32[]{:S(2)}) collective-permute-start(bf16[72,128]{1,0:T(8,128)(2,1)S(1)} %get-tuple-element.25.refs_0_), channel_id=1, source_target_pairs={{0,2},{2,0},{4,6},{6,4},{1,3},{3,1},{5,7},{7,5},{8,10},{10,8},{12,... | collective-permute-start | bytes 55304 | tf_op jit(solution)/shard_map/ppermute | solution.py:17
  10.6 1.6 %collective-permute-start.8 = (bf16[72,128]{1,0:T(8,128)(2,1)S(1)}, bf16[72,128]{1,0:T(8,128)(2,1)S(1)}, u32[]{:S(2)}, u32[]{:S(2)}) collective-permute-start(bf16[72,128]{1,0:T(8,128)(2,1)S(1)} %collective-permute-done.6.refs_1_), channel_id=1, source_target_pairs={{0,2},{2,0},{4,6},{6,4},{1,3},{3,1},{5,7},{7,5},{8,10},{10,8},{12,... | collective-permute-start | bytes 55304 | tf_op jit(solution)/shard_map/ppermute | solution.py:17
  11.1 1.6 %collective-permute-start.3 = (bf16[72,128]{1,0:T(8,128)(2,1)S(1)}, bf16[72,128]{1,0:T(8,128)(2,1)S(1)}, u32[]{:S(2)}, u32[]{:S(2)}) collective-permute-start(bf16[72,128]{1,0:T(8,128)(2,1)S(1)} %collective-permute-done.2.refs_2_), channel_id=1, source_target_pairs={{0,2},{2,0},{4,6},{6,4},{1,3},{3,1},{5,7},{7,5},{8,10},{10,8},{12,... | collective-permute-start | bytes 55304 | tf_op jit(solution)/shard_map/ppermute | solution.py:17
  11.2 1.4 %collective-permute-start.5 = (bf16[72,128]{1,0:T(8,128)(2,1)S(1)}, bf16[72,128]{1,0:T(8,128)(2,1)S(1)}, u32[]{:S(2)}, u32[]{:S(2)}) collective-permute-start(bf16[72,128]{1,0:T(8,128)(2,1)S(1)} %collective-permute-done.4.refs_3_), channel_id=1, source_target_pairs={{0,2},{2,0},{4,6},{6,4},{1,3},{3,1},{5,7},{7,5},{8,10},{10,8},{12,... | collective-permute-start | bytes 55304 | tf_op jit(solution)/shard_map/ppermute | solution.py:17
  12.8 3.3 %collective-permute-start.10 = (bf16[96,128]{1,0:T(8,128)(2,1)S(1)}, bf16[96,128]{1,0:T(8,128)(2,1)S(1)}, u32[]{:S(2)}, u32[]{:S(2)}) collective-permute-start(bf16[96,128]{1,0:T(8,128)(2,1)S(1)} %get-tuple-element.29), channel_id=1, source_target_pairs={{0,6},{2,4},{4,2},{6,0},{1,7},{3,5},{5,3},{7,1},{8,14},{10,12},{12... | collective-permute-start | bytes 73736 | tf_op jit(solution)/shard_map/ppermute | solution.py:17
  13.2 3.9 %collective-permute-start.11 = (bf16[96,128]{1,0:T(8,128)(2,1)S(1)}, bf16[96,128]{1,0:T(8,128)(2,1)S(1)}, u32[]{:S(2)}, u32[]{:S(2)}) collective-permute-start(bf16[96,128]{1,0:T(8,128)(2,1)S(1)} %get-tuple-element.30), channel_id=1, source_target_pairs={{0,7},{1,2},{2,5},{3,0},{4,3},{5,6},{6,1},{7,4},{8,15},{9,10},{10,... | collective-permute-start | bytes 73736 | tf_op jit(solution)/shard_map/ppermute | solution.py:338
  15.6 4.2 %collective-permute-start.9 = (bf16[96,128]{1,0:T(8,128)(2,1)S(1)}, bf16[96,128]{1,0:T(8,128)(2,1)S(1)}, u32[]{:S(2)}, u32[]{:S(2)}) collective-permute-start(bf16[96,128]{1,0:T(8,128)(2,1)S(1)} %get-tuple-element.28), channel_id=1, source_target_pairs={{0,3},{1,6},{2,1},{3,4},{4,7},{5,2},{6,5},{7,0},{8,11},{9,14},{10,... | collective-permute-start | bytes 73736 | tf_op jit(solution)/shard_map/ppermute | solution.py:336

commit v5 on v4

--- a/solution.py
+++ b/solution.py
@@ -183,7 +183,7 @@
 
 
 def sum_kernel(dims, parts, *refs):
-    block_refs, (table_ref, before_ref, total_ref, soon_ref, y_ref, late_ref, rows_ref) = refs[:-7], refs[-7:]
+    block_refs, (table_ref, before_ref, total_ref, soon_ref, y_ref, late_ref, rows_ref, packed_ref) = refs[:-8], refs[-8:]
     for i, block_ref in enumerate(block_refs):
         rows_ref[i] = block_ref[...].astype(F32)
     for p in range(2):
@@ -192,19 +192,26 @@
         for i, total in enumerate(totals):
             total_ref[2 * i + p] = total
     group = lax.axis_index("grp")
-    for at, ref in ((16 * group, soon_ref), (8, y_ref), (16 - 16 * group, late_ref)):
-        ref[...] = total_ref[:, pl.ds(pl.multiple_of(at, 8), 8), :].reshape(ref.shape).astype(BF16)
-
-
-def finish_kernel(dims, weights_ref, slot_lanes_ref, total_ref, soon_ref, y_ref, late_ref, out_hbm, temps_ref, rows_ref, out_ref, sems):
+    halves = packed_ref.shape[1] // total_ref.shape[0]
+    for i, (at, ref) in enumerate(((16 * group, soon_ref), (8, y_ref), (16 - 16 * group, late_ref))):
+        for n in range(total_ref.shape[0]):
+            packed_ref[i, n * halves : (n + 1) * halves] = total_ref[n, pl.ds(pl.multiple_of(at, 8), halves), :]
+        ref[...] = packed_ref[i].astype(BF16)
+
+
+def finish_kernel(dims, weights_ref, slot_lanes_ref, total_ref, soon_ref, y_ref, late_ref, out_hbm, temps_ref, rows_ref, out_ref, given_ref, sems):
     fields, levels, halves, slots, waves = dims
     planes = 2 * (levels // 4)
     width = LANES // planes
     lev, group = lax.axis_index("lev"), lax.axis_index("grp")
     y, core = lev // 2, lev % 2
     count = 4 * fields
-    soon, from_y, late = (r[...].astype(F32).reshape(count, 8, LANES) for r in (soon_ref, y_ref, late_ref))
-    from_x, from_xy = jnp.where(group == 0, late, soon), jnp.where(group == 0, soon, late)
+    for i, ref in enumerate((soon_ref, y_ref, late_ref)):
+        given_ref[i, : count * halves] = ref[...].astype(F32)
+
+    def given(i, n):
+        return given_ref[i, n * halves : n * halves + 8, :]
+
     half = (lev * 2 + group) * halves + iota((8, LANES), 0)
     field_rows = levels * halves * 2
     copies = []
@@ -230,7 +237,7 @@
                     [total_ref[n, 6:8, :], total_ref[n, 14:16, :], total_ref[n, 22:24, :], jnp.zeros((2, LANES), F32)],
                     axis=0,
                 )
-                for far, value in enumerate((kept + from_x[far_n], from_y[far_n] + from_xy[far_n])):
+                for far, value in enumerate((kept + given(2 - 2 * group, far_n), given(1, far_n) + given(2 * group, far_n))):
                     value = jnp.where(valid, value, 0.0)
                     first = ((y ^ far) * 2 + (core ^ side)) * (levels // 4)
                     for plane in range(planes):
@@ -309,7 +316,7 @@
         other[k] = flipped(own[k], "lev", 1)
 
     count = 4 * fields
-    message = shape((count * 8, LANES), BF16)
+    message = shape((count * (halves // 2), LANES), BF16)
     totals = shape((count, 24, LANES), F32)
     parts = [(own[k], (min(k, 1), k)) for k in range(bands)] + [(other[k], (1 - min(k, 1), k)) for k in range(bands)]
     early, others = parts[: bands + 2], parts[bands + 2 :]
@@ -327,7 +334,10 @@
         in_specs=[VMEM] * (len(others) + 2),
         out_specs=[VMEM] * 4,
         out_shape=[totals] + [message] * 3,
-        scratch_shapes=[pltpu.VMEM((max(len(others), 1), *block.shape), F32)],
+        scratch_shapes=[
+            pltpu.VMEM((max(len(others), 1), *block.shape), F32),
+            pltpu.VMEM((3, *message.shape), F32),
+        ],
         compiler_params=pltpu.CompilerParams(vmem_limit_bytes=GRANT),
         name="sum",
     )(*[value for value, _ in others], table, before)
@@ -347,6 +357,7 @@
             pltpu.VMEM((levels, 4, 8, LANES), F32),
             pltpu.VMEM((out_rows + 16, LANES), F32),
             pltpu.VMEM((out_rows, slots), BF16),
+            pltpu.VMEM((3, message.shape[0] + 8, LANES), F32),
             pltpu.SemaphoreType.DMA((4,)),
         ],
         compiler_params=pltpu.CompilerParams(vmem_limit_bytes=GRANT),

time: 20.7 us -> 20.7 us (level)
  no operation moved by 1% of the time
where the time goes in v5:
time: 20.7 us; the launch traced here: 20.5 us
  starting transfers between devices  10.9 us (53%)
  waiting for transfers between devices  6.4 us (31%)
  Pallas kernels  3.13 us (15%)
    ppermute x7, starting transfers between devices, flipped(): lax.ppermute(value, axis, [(i, i ^ step) for i in range(lax.axis_size(axi...  4.66 us
    ppermute x3, starting transfers between devices, fast_body(): own[k] = lax.ppermute(blocks[k], ('band', 'lev'), crossed(k))  3.88 us
    ppermute x1, waiting for transfers between devices, fast_body(): from_soon = lax.ppermute(soon, ('lev', 'grp'), round_the_square(levs, 0))  2.62 us
    ppermute x1, starting transfers between devices, fast_body(): from_late = lax.ppermute(late, ('lev', 'grp'), round_the_square(levs, 1))  2.38 us
    ppermute x3, waiting for transfers between devices, fast_body(): own[k] = lax.ppermute(blocks[k], ('band', 'lev'), crossed(k))  2.31 us
    pallas_call x1, Pallas kernels, fast_body(): pl.pallas_call(functools.partial(prepare_kernel, (fields, planes, pairs,...  1.06 us
    ppermute x1, waiting for transfers between devices, fast_body(): from_late = lax.ppermute(late, ('lev', 'grp'), round_the_square(levs, 1))  0.95 us
    pallas_call x1, Pallas kernels, fast_body(): pl.pallas_call(functools.partial(finish_kernel, (fields, levels, own_halv...  0.88 us
  transfers between devices with their start and end apart: 12, of which 5 were waited for; matrix products, arithmetic and copies ran while one was open for 0% of the time, Pallas kernels for 5%

profile of v5, /device:TPU:0, one launch (start us, length us, event | category | flops | bytes accessed | tf_op | source)
XLA Modules:
  0.0 20.5 jit_solution(16711033165679048398)
XLA Ops:
  0.0 1.1 %prepare.1 = (s32[8,128]{1,0:T(8,128)S(1)}, bf16[576,48]{1,0:T(8,128)(2,1)S(1)}, f32[8,8]{1,0:T(8,128)S(1)}, bf16[72,128]{1,0:T(8,128)(2,1)S(1)}, bf16[72,128]{1...) custom-call(s32[1,12]{1,0:T(1,128)} %lat_hbm.1, s32[1,96]{1,0:T(1,128)} %bitcast.13, ...), custom_call_target="tpu_custom_call" | custom-call | tf_op jit(solution)/shard_map/prepare/pallas_call | solution.py:280
  1.1 0.6 %collective-permute-start = (bf16[576,48]{1,0:T(8,128)(2,1)S(1)}, bf16[576,48]{1,0:T(8,128)(2,1)S(1)}, u32[]{:S(2)}, u32[]{:S(2)}) collective-permute-start(bf16[576,48]{1,0:T(8,128)(2,1)S(1)} %get-tuple-element.18.own_ref), channel_id=1, source_target_pairs={{0,2},{2,0},{4,6},{6,4},{1,3},{3,1},{5,7},{7,5},{8,10},{10,8},{12,... | collective-permute-start | bytes 165896 | tf_op jit(solution)/shard_map/ppermute | solution.py:17
  1.6 2.6 %collective-permute-start.1 = (bf16[576,48]{1,0:T(8,128)(2,1)}, bf16[576,48]{1,0:T(8,128)(2,1)S(1)}, u32[]{:S(2)}, u32[]{:S(2)}) collective-permute-start(bf16[576,48]{1,0:T(8,128)(2,1)} %bitcast.11), channel_id=1, source_target_pairs={{0,6},{2,4},{4,2},{6,0},{1,7},{3,5},{5,3},{7,1},{8,14},{10,12},{12... | collective-permute-start | bytes 165896 | tf_op jit(solution)/shard_map/ppermute | solution.py:17
  4.3 2.3 %collective-permute-start.6 = (bf16[72,128]{1,0:T(8,128)(2,1)S(1)}, bf16[72,128]{1,0:T(8,128)(2,1)S(1)}, u32[]{:S(2)}, u32[]{:S(2)}) collective-permute-start(bf16[72,128]{1,0:T(8,128)(2,1)S(1)} %get-tuple-element.26), channel_id=1, source_target_pairs={{0,18},{2,16},{4,22},{6,20},{8,26},{10,24},{12,30},{14,28},{16,10}... | collective-permute-start | bytes 55304 | tf_op jit(solution)/shard_map/ppermute | solution.py:303
  6.5 1.3 %collective-permute-start.2 = (bf16[72,128]{1,0:T(8,128)(2,1)S(1)}, bf16[72,128]{1,0:T(8,128)(2,1)S(1)}, u32[]{:S(2)}, u32[]{:S(2)}) collective-permute-start(bf16[72,128]{1,0:T(8,128)(2,1)S(1)} %get-tuple-element.22), channel_id=1, source_target_pairs={{0,26},{2,24},{4,30},{6,28},{8,18},{10,16},{12,22},{14,20},{16,2},... | collective-permute-start | bytes 55304 | tf_op jit(solution)/shard_map/ppermute | solution.py:303
  7.8 0.3 %collective-permute-start.4 = (bf16[72,128]{1,0:T(8,128)(2,1)S(1)}, bf16[72,128]{1,0:T(8,128)(2,1)S(1)}, u32[]{:S(2)}, u32[]{:S(2)}) collective-permute-start(bf16[72,128]{1,0:T(8,128)(2,1)S(1)} %get-tuple-element.23), channel_id=1, source_target_pairs={{0,10},{2,8},{4,14},{6,12},{8,2},{10,0},{12,6},{14,4},{16,26},{18,... | collective-permute-start | bytes 55304 | tf_op jit(solution)/shard_map/ppermute | solution.py:303
  8.1 1.1 %collective-permute-done.6.refs_1_ = bf16[72,128]{1,0:T(8,128)(2,1)S(1)} collective-permute-done((bf16[72,128]{1,0:T(8,128)(2,1)S(1)}, bf16[72,128]{1,0:T(8,128)(2,1)S(1)}, u32[]{:S(2)}, u32[]{:S(2)}) %collective-permute-start.6) | collective-permute-done | bytes 18464 | tf_op jit(solution)/shard_map/ppermute | solution.py:303
  9.2 0.2 collective-permute-start.7
  9.4 1.2 %collective-permute-done.2.refs_2_ = bf16[72,128]{1,0:T(8,128)(2,1)S(1)} collective-permute-done((bf16[72,128]{1,0:T(8,128)(2,1)S(1)}, bf16[72,128]{1,0:T(8,128)(2,1)S(1)}, u32[]{:S(2)}, u32[]{:S(2)}) %collective-permute-start.2) | collective-permute-done | bytes 18464 | tf_op jit(solution)/shard_map/ppermute | solution.py:303
  10.6 0.4 %collective-permute-start.8 = (bf16[72,128]{1,0:T(8,128)(2,1)S(1)}, bf16[72,128]{1,0:T(8,128)(2,1)S(1)}, u32[]{:S(2)}, u32[]{:S(2)}) collective-permute-start(bf16[72,128]{1,0:T(8,128)(2,1)S(1)} %collective-permute-done.6.refs_1_), channel_id=1, source_target_pairs={{0,2},{2,0},{4,6},{6,4},{1,3},{3,1},{5,7},{7,5},{8,10},{10,8},{12,... | collective-permute-start | bytes 55304 | tf_op jit(solution)/shard_map/ppermute | solution.py:17
  11.0 0.0 collective-permute-done.4.refs_3_
  11.1 0.2 collective-permute-start.3
  11.2 0.0 collective-permute-done.core_ref
  11.2 0.3 %collective-permute-start.5 = (bf16[72,128]{1,0:T(8,128)(2,1)S(1)}, bf16[72,128]{1,0:T(8,128)(2,1)S(1)}, u32[]{:S(2)}, u32[]{:S(2)}) collective-permute-start(bf16[72,128]{1,0:T(8,128)(2,1)S(1)} %collective-permute-done.4.refs_3_), channel_id=1, source_target_pairs={{0,2},{2,0},{4,6},{6,4},{1,3},{3,1},{5,7},{7,5},{8,10},{10,8},{12,... | collective-permute-start | bytes 55304 | tf_op jit(solution)/shard_map/ppermute | solution.py:17
  11.6 0.0 collective-permute-done.1.other_ref
  11.6 0.6 %spread.1 = (f32[2,1152,128]{2,1,0:T(8,128)S(1)}, f32[64,8,128]{2,1,0:T(8,128)S(1)}) custom-call(bf16[576,48]{1,0:T(8,128)(2,1)S(1)} %get-tuple-element.18.own_ref, bf16[576,48]{1,0:T(8,128)(2,1)S(1)} %collective-permute-done.core_ref, bf16[576,48]{1,0:T(8,128)(2,1)S(1)} %collective-permute-done.1.other_ref, f32[8,8]{1,0:T(8,128)S(1)} %get-tuple-element.19.vertical_ref), custom_call_target="tpu_custom_call" | custom-call | tf_op jit(solution)/shard_map/spread/pallas_call | solution.py:305
  12.2 0.0 collective-permute-done.7.refs_4_
  12.2 0.0 collective-permute-done.8.refs_5_
  12.2 0.4 %sum_first.1.refs_3_ = f32[12,24,128]{2,1,0:T(8,128)S(1)} custom-call(bf16[72,128]{1,0:T(8,128)(2,1)S(1)} %get-tuple-element.25.refs_0_, bf16[72,128]{1,0:T(8,128)(2,1)S(1)} %collective-permute-done.6.refs_1_, bf16[72,128]{1,0:T(8,128)(2,1)S(1)} %collective-permute-done.2.refs_2_, bf16[72,128]{1,0:T(8,128)(2,1)S(1)} %collective-permute-done.4.refs_3_, ...), custom_call_target="tpu_custom_call" | custom-call | tf_op jit(solution)/shard_map/sum_first/pallas_call | solution.py:323
  12.6 0.0 collective-permute-done.3.refs_0_
  12.6 0.0 collective-permute-done.5.refs_1_
  12.7 0.2 sum.1
  12.8 0.4 %collective-permute-start.10 = (bf16[72,128]{1,0:T(8,128)(2,1)S(1)}, bf16[72,128]{1,0:T(8,128)(2,1)S(1)}, u32[]{:S(2)}, u32[]{:S(2)}) collective-permute-start(bf16[72,128]{1,0:T(8,128)(2,1)S(1)} %get-tuple-element.29), channel_id=1, source_target_pairs={{0,6},{2,4},{4,2},{6,0},{1,7},{3,5},{5,3},{7,1},{8,14},{10,12},{12... | collective-permute-start | bytes 55304 | tf_op jit(solution)/shard_map/ppermute | solution.py:17
  13.2 2.4 %collective-permute-start.11 = (bf16[72,128]{1,0:T(8,128)(2,1)S(1)}, bf16[72,128]{1,0:T(8,128)(2,1)S(1)}, u32[]{:S(2)}, u32[]{:S(2)}) collective-permute-start(bf16[72,128]{1,0:T(8,128)(2,1)S(1)} %get-tuple-element.30), channel_id=1, source_target_pairs={{0,7},{1,2},{2,5},{3,0},{4,3},{5,6},{6,1},{7,4},{8,15},{9,10},{10,... | collective-permute-start | bytes 55304 | tf_op jit(solution)/shard_map/ppermute | solution.py:348
  15.6 0.0 collective-permute-start.9
  15.6 0.5 %collective-permute-done.10.y_ref = bf16[72,128]{1,0:T(8,128)(2,1)S(1)} collective-permute-done((bf16[72,128]{1,0:T(8,128)(2,1)S(1)}, bf16[72,128]{1,0:T(8,128)(2,1)S(1)}, u32[]{:S(2)}, u32[]{:S(2)}) %collective-permute-start.10) | collective-permute-done | bytes 18464 | tf_op jit(solution)/shard_map/ppermute | solution.py:17
  16.1 1.0 %collective-permute-done.11.late_ref = bf16[72,128]{1,0:T(8,128)(2,1)S(1)} collective-permute-done((bf16[72,128]{1,0:T(8,128)(2,1)S(1)}, bf16[72,128]{1,0:T(8,128)(2,1)S(1)}, u32[]{:S(2)}, u32[]{:S(2)}) %collective-permute-start.11) | collective-permute-done | bytes 18464 | tf_op jit(solution)/shard_map/ppermute | solution.py:348
  17.0 2.6 %collective-permute-done.9.soon_ref = bf16[72,128]{1,0:T(8,128)(2,1)S(1)} collective-permute-done((bf16[72,128]{1,0:T(8,128)(2,1)S(1)}, bf16[72,128]{1,0:T(8,128)(2,1)S(1)}, u32[]{:S(2)}, u32[]{:S(2)}) %collective-permute-start.9) | collective-permute-done | bytes 18464 | tf_op jit(solution)/shard_map/ppermute | solution.py:346
  19.6 0.9 %finish.1 = bf16[768,24]{1,0:T(8,128)(2,1)} custom-call(f32[64,8,128]{2,1,0:T(8,128)S(1)} %get-tuple-element.20.weights_ref, s32[8,128]{1,0:T(8,128)S(1)} %get-tuple-element.21.slot_lanes_ref, f32[12,24,128]{2,1,0:T(8,128)S(1)} %get-tuple-element.27.total_ref, bf16[72,128]{1,0:T(8,128)(2,1)S(1)} %collective-permute-done.9.soon_ref, ...), custom_call_target="tpu_custom_call" | custom-call | tf_op jit(solution)/shard_map/finish/pallas_call | solution.py:351
Async XLA Ops:
  1.1 10.2 %collective-permute-start = (bf16[576,48]{1,0:T(8,128)(2,1)S(1)}, bf16[576,48]{1,0:T(8,128)(2,1)S(1)}, u32[]{:S(2)}, u32[]{:S(2)}) collective-permute-start(bf16[576,48]{1,0:T(8,128)(2,1)S(1)} %get-tuple-element.18.own_ref), channel_id=1, source_target_pairs={{0,2},{2,0},{4,6},{6,4},{1,3},{3,1},{5,7},{7,5},{8,10},{10,8},{12,... | collective-permute-start | bytes 165896 | tf_op jit(solution)/shard_map/ppermute | solution.py:17
  1.6 9.9 %collective-permute-start.1 = (bf16[576,48]{1,0:T(8,128)(2,1)}, bf16[576,48]{1,0:T(8,128)(2,1)S(1)}, u32[]{:S(2)}, u32[]{:S(2)}) collective-permute-start(bf16[576,48]{1,0:T(8,128)(2,1)} %bitcast.11), channel_id=1, source_target_pairs={{0,6},{2,4},{4,2},{6,0},{1,7},{3,5},{5,3},{7,1},{8,14},{10,12},{12... | collective-permute-start | bytes 165896 | tf_op jit(solution)/shard_map/ppermute | solution.py:17
  4.3 5.0 %collective-permute-start.6 = (bf16[72,128]{1,0:T(8,128)(2,1)S(1)}, bf16[72,128]{1,0:T(8,128)(2,1)S(1)}, u32[]{:S(2)}, u32[]{:S(2)}) collective-permute-start(bf16[72,128]{1,0:T(8,128)(2,1)S(1)} %get-tuple-element.26), channel_id=1, source_target_pairs={{0,18},{2,16},{4,22},{6,20},{8,26},{10,24},{12,30},{14,28},{16,10}... | collective-permute-start | bytes 55304 | tf_op jit(solution)/shard_map/ppermute | solution.py:303
  6.5 4.1 %collective-permute-start.2 = (bf16[72,128]{1,0:T(8,128)(2,1)S(1)}, bf16[72,128]{1,0:T(8,128)(2,1)S(1)}, u32[]{:S(2)}, u32[]{:S(2)}) collective-permute-start(bf16[72,128]{1,0:T(8,128)(2,1)S(1)} %get-tuple-element.22), channel_id=1, source_target_pairs={{0,26},{2,24},{4,30},{6,28},{8,18},{10,16},{12,22},{14,20},{16,2},... | collective-permute-start | bytes 55304 | tf_op jit(solution)/shard_map/ppermute | solution.py:303
  7.8 3.3 %collective-permute-start.4 = (bf16[72,128]{1,0:T(8,128)(2,1)S(1)}, bf16[72,128]{1,0:T(8,128)(2,1)S(1)}, u32[]{:S(2)}, u32[]{:S(2)}) collective-permute-start(bf16[72,128]{1,0:T(8,128)(2,1)S(1)} %get-tuple-element.23), channel_id=1, source_target_pairs={{0,10},{2,8},{4,14},{6,12},{8,2},{10,0},{12,6},{14,4},{16,26},{18,... | collective-permute-start | bytes 55304 | tf_op jit(solution)/shard_map/ppermute | solution.py:303
  9.2 3.0 %collective-permute-start.7 = (bf16[72,128]{1,0:T(8,128)(2,1)S(1)}, bf16[72,128]{1,0:T(8,128)(2,1)S(1)}, u32[]{:S(2)}, u32[]{:S(2)}) collective-permute-start(bf16[72,128]{1,0:T(8,128)(2,1)S(1)} %get-tuple-element.25.refs_0_), channel_id=1, source_target_pairs={{0,2},{2,0},{4,6},{6,4},{1,3},{3,1},{5,7},{7,5},{8,10},{10,8},{12,... | collective-permute-start | bytes 55304 | tf_op jit(solution)/shard_map/ppermute | solution.py:17
  10.6 1.6 %collective-permute-start.8 = (bf16[72,128]{1,0:T(8,128)(2,1)S(1)}, bf16[72,128]{1,0:T(8,128)(2,1)S(1)}, u32[]{:S(2)}, u32[]{:S(2)}) collective-permute-start(bf16[72,128]{1,0:T(8,128)(2,1)S(1)} %collective-permute-done.6.refs_1_), channel_id=1, source_target_pairs={{0,2},{2,0},{4,6},{6,4},{1,3},{3,1},{5,7},{7,5},{8,10},{10,8},{12,... | collective-permute-start | bytes 55304 | tf_op jit(solution)/shard_map/ppermute | solution.py:17
  11.1 1.6 %collective-permute-start.3 = (bf16[72,128]{1,0:T(8,128)(2,1)S(1)}, bf16[72,128]{1,0:T(8,128)(2,1)S(1)}, u32[]{:S(2)}, u32[]{:S(2)}) collective-permute-start(bf16[72,128]{1,0:T(8,128)(2,1)S(1)} %collective-permute-done.2.refs_2_), channel_id=1, source_target_pairs={{0,2},{2,0},{4,6},{6,4},{1,3},{3,1},{5,7},{7,5},{8,10},{10,8},{12,... | collective-permute-start | bytes 55304 | tf_op jit(solution)/shard_map/ppermute | solution.py:17
  11.2 1.4 %collective-permute-start.5 = (bf16[72,128]{1,0:T(8,128)(2,1)S(1)}, bf16[72,128]{1,0:T(8,128)(2,1)S(1)}, u32[]{:S(2)}, u32[]{:S(2)}) collective-permute-start(bf16[72,128]{1,0:T(8,128)(2,1)S(1)} %collective-permute-done.4.refs_3_), channel_id=1, source_target_pairs={{0,2},{2,0},{4,6},{6,4},{1,3},{3,1},{5,7},{7,5},{8,10},{10,8},{12,... | collective-permute-start | bytes 55304 | tf_op jit(solution)/shard_map/ppermute | solution.py:17
  12.8 3.3 %collective-permute-start.10 = (bf16[72,128]{1,0:T(8,128)(2,1)S(1)}, bf16[72,128]{1,0:T(8,128)(2,1)S(1)}, u32[]{:S(2)}, u32[]{:S(2)}) collective-permute-start(bf16[72,128]{1,0:T(8,128)(2,1)S(1)} %get-tuple-element.29), channel_id=1, source_target_pairs={{0,6},{2,4},{4,2},{6,0},{1,7},{3,5},{5,3},{7,1},{8,14},{10,12},{12... | collective-permute-start | bytes 55304 | tf_op jit(solution)/shard_map/ppermute | solution.py:17
  13.2 3.8 %collective-permute-start.11 = (bf16[72,128]{1,0:T(8,128)(2,1)S(1)}, bf16[72,128]{1,0:T(8,128)(2,1)S(1)}, u32[]{:S(2)}, u32[]{:S(2)}) collective-permute-start(bf16[72,128]{1,0:T(8,128)(2,1)S(1)} %get-tuple-element.30), channel_id=1, source_target_pairs={{0,7},{1,2},{2,5},{3,0},{4,3},{5,6},{6,1},{7,4},{8,15},{9,10},{10,... | collective-permute-start | bytes 55304 | tf_op jit(solution)/shard_map/ppermute | solution.py:348
  15.6 4.1 %collective-permute-start.9 = (bf16[72,128]{1,0:T(8,128)(2,1)S(1)}, bf16[72,128]{1,0:T(8,128)(2,1)S(1)}, u32[]{:S(2)}, u32[]{:S(2)}) collective-permute-start(bf16[72,128]{1,0:T(8,128)(2,1)S(1)} %get-tuple-element.28), channel_id=1, source_target_pairs={{0,3},{1,6},{2,1},{3,4},{4,7},{5,2},{6,5},{7,0},{8,11},{9,14},{10,... | collective-permute-start | bytes 55304 | tf_op jit(solution)/shard_map/ppermute | solution.py:346
